TPU v7x, 32 devices: a whole 2x2x4 slice. The times are simulated.
32 devices in a mesh: dp: 8 (over y, x, core), fsdp: 4 (over z).
Axes of the slice: x: 2, y: 2, z: 4, core: 2. Of those that a mesh axis runs over, the one named last changes fastest.
Arguments:
- img_emb: bfloat16 [1024, 1024], P(('dp', 'fsdp')), may hold values from -0.25 to 0.25
- txt_emb: bfloat16 [1024, 1024], P(('dp', 'fsdp')), may hold values from -0.25 to 0.25
- img_ids: int32 [1024], P(('dp', 'fsdp')), may hold values from 0 to 1023
- txt_ids: int32 [1024], P(('dp', 'fsdp')), may hold values from 0 to 1023
- temp_log: float32 [1], replicated, may hold values from 1.5 to 2.5
- logit_bias: float32 [1], replicated, may hold values from -6 to -2
- block_in: bfloat16 [2048, 3072], P(('dp', 'fsdp')), may hold values from -6 to 6
- dw_kernel: float32 [49, 3072], replicated, may hold values from -0.875 to 0.875
- ln_gain: float32 [3072], replicated, may hold values from 0.5 to 1.5
- ln_bias: float32 [3072], replicated, may hold values from -3 to 3
- w_up: bfloat16 [3072, 6144], P(None, 'fsdp'), may hold values from -0.109375 to 0.109375
- w_down: bfloat16 [6144, 3072], P('fsdp'), may hold values from -0.078125 to 0.078125
- layer_scale: float32 [3072], replicated, may hold values from 0.1 to 1
- head_gain: float32 [3072], replicated, may hold values from 0.5 to 1.5
- head_bias: float32 [3072], replicated, may hold values from -3 to 3
- w_proj: bfloat16 [3072, 1024], replicated, may hold values from -0.109375 to 0.109375
Outputs:
- img_grad: float32 [1024, 1024], P(('dp', 'fsdp'))
- txt_grad: float32 [1024, 1024], P(('dp', 'fsdp'))
- w_up_grad: float32 [3072, 6144], P('dp', 'fsdp')
- w_down_grad: float32 [6144, 3072], P('fsdp', 'dp')
All inputs are finite; a program needn't handle non-finite values.
Results may differ from a plain program's by a relative error of at most 0.02.
Values may be sent and summed in bfloat16 or wider, within the bound.
A program may use at most 128 MiB of HBM per device.

v0:
```python
import functools

import jax
import jax.numpy as jnp
from jax import lax
from jax.experimental import pallas as pl
from jax.experimental.pallas import tpu as pltpu
from jax.sharding import PartitionSpec as P

KERNEL = 7
SIDE = 8


def unit_rows(matrix):
    values = matrix.astype(jnp.float32)
    length = jnp.sqrt(jnp.sum(values * values, axis=1, keepdims=True) + 1e-06)
    return (values / length, length)


def back_unit(gradient, unit_part, length):
    inner_prod = jnp.sum(unit_part * gradient, axis=1, keepdims=True)
    return (gradient - unit_part * inner_prod) / length


def depthwise(pictures, kernel):
    reach = KERNEL // 2
    padded = jnp.pad(pictures, ((0, 0), (reach, reach), (reach, reach), (0, 0)))
    summed = jnp.zeros_like(pictures)
    for above in range(KERNEL):
        for across in range(KERNEL):
            summed = (
                summed
                + kernel[above * KERNEL + across]
                * padded[:, above : above + SIDE, across : across + SIDE, :]
            )
    return summed


def layer_norm(values, gain_vec, bias_vec):
    centre = jnp.mean(values, axis=-1, keepdims=True)
    centred = values - centre
    inverse = 1.0 / jnp.sqrt(jnp.mean(centred * centred, axis=-1, keepdims=True) + 1e-06)
    normal = centred * inverse
    return (normal * gain_vec + bias_vec, normal, inverse)


MESH = pl.DeviceIdType.MESH
VMEM = pl.BlockSpec(memory_space=pltpu.VMEM)
ANY = pl.BlockSpec(memory_space=pl.ANY)


def greet_peers(n_dp, n_fsdp):
    d, f = lax.axis_index("dp"), lax.axis_index("fsdp")
    barrier = pltpu.get_barrier_semaphore()
    for k in range(1, n_dp):
        pl.semaphore_signal(barrier, inc=1, device_id={"dp": (d + k) % n_dp}, device_id_type=MESH)
    for k in range(1, n_fsdp):
        pl.semaphore_signal(barrier, inc=1, device_id={"fsdp": (f + k) % n_fsdp}, device_id_type=MESH)
    pl.semaphore_wait(barrier, n_dp + n_fsdp - 2)


def push(source, target, send_sem, recv_sem, **peer):
    return pltpu.make_async_remote_copy(
        src_ref=source,
        dst_ref=target,
        send_sem=send_sem,
        recv_sem=recv_sem,
        device_id=peer,
        device_id_type=MESH,
    )


def second_parts(x):
    cubic = 0.044715
    slant = 0.7978845608028654
    square = x * x
    t = jnp.tanh(slant * x * (1.0 + cubic * square))
    half = 0.5 * (1.0 + t)
    slope = half + 0.5 * x * (1.0 - t * t) * slant * (1.0 + 3.0 * cubic * square)
    return x * half, slope


def nt_dot(left, right):
    return lax.dot_general(
        left, right, (((1,), (1,)), ((), ())), preferred_element_type=jnp.float32
    )


def whole_kernel(
    n_dp, n_fsdp, spread, norm, img, txt, temper, offset, means, scale, gain, bias,
    up_hbm, down_hbm, proj_hbm,
    grp, own, all_slope, all_grad, all_act, img_sum, txt_sum,
    up, down, proj, gimg, ctxt, slope, crit, imgs, txts, crit_in, imgs_in, txts_in, lines, partial,
    *sems,
):
    (
        loc, txt_s, txt_r, img_s, img_r, rgt_s, rgt_r, lft_s, lft_r, col_s, col_r, col_l,
        slo_l, slo_s, slo_r, fwd_s, fwd_r, cri_s, cri_r, ims_s, ims_r, txs_s, txs_r,
        act_s, act_r, gra_s, gra_r, grd_s, grd_r,
    ) = sems
    d, f = lax.axis_index("dp"), lax.axis_index("fsdp")
    rows, channels = norm.shape
    share = channels // n_dp
    embed_width = proj.shape[1]
    hid_width = up.shape[1]
    pairs = img.shape[0]
    partner = d + 1 - 2 * (d % 2)
    keep = [
        pltpu.make_async_copy(up_hbm, up, loc.at[0]),
        pltpu.make_async_copy(norm, grp.at[f], loc.at[1]),
        pltpu.make_async_copy(img, gimg.at[f], loc.at[2]),
        pltpu.make_async_copy(txt, ctxt.at[d], loc.at[3]),
        pltpu.make_async_copy(down_hbm, down, loc.at[4]),
        pltpu.make_async_copy(proj_hbm, proj, loc.at[5]),
    ]
    for copy in keep:
        copy.start()
    greet_peers(n_dp, n_fsdp)

    def right(h, source, b):
        return push(source, grp.at[b], rgt_s.at[h], rgt_r.at[h], fsdp=f + 1)

    def left(h, source, b):
        return push(source, grp.at[b], lft_s.at[h], lft_r.at[h], fsdp=f - 1)

    def columns(source, owner):
        return source.at[:, pl.ds(pl.multiple_of(owner * share, 128), share)]

    def column_copy(k, source, b):
        peer = (d + k) % n_dp
        return push(columns(source, peer), own.at[d, b], col_s.at[b, k - 1], col_r.at[b, k - 1], dp=peer)

    def scatter(source, b):
        if spread:
            for k in range(1, n_dp):
                column_copy(k, source, b).start()
            pltpu.make_async_copy(columns(source, d), own.at[d, b], col_l.at[b]).start()

    def slope_copy(k, b):
        peer = partner if k == 0 else (d + k) % n_dp
        return push(slope.at[b], all_slope.at[d, b], slo_s.at[b, k // 2], slo_r.at[b, k // 2], dp=peer)

    def slope_keep(b):
        return pltpu.make_async_copy(slope.at[b], all_slope.at[d, b], slo_l.at[b])

    def onward(k, b):
        spot = all_slope.at[(d + n_dp - k) % n_dp, b]
        return push(spot, spot, fwd_s.at[b, k // 2], fwd_r.at[b, k // 2], dp=partner)

    wide = 256 if hid_width % 256 == 0 else 128

    def expand(source, b):
        def tile(i, carry):
            cols = pl.ds(pl.multiple_of(i * wide, wide), wide)
            hidden = jnp.dot(source[...], up[:, cols], preferred_element_type=jnp.float32)
            active, slant = second_parts(hidden)
            slope[b, :, cols] = slant.astype(jnp.bfloat16)
            active = active.astype(jnp.bfloat16).astype(jnp.float32)
            all_act[d, b, :, cols] = jnp.sum(active, axis=0, keepdims=True)
            return carry

        lax.fori_loop(0, hid_width // wide, tile, 0)
        for k in range(0, n_dp, 2):
            slope_copy(k, b).start()
        slope_keep(b).start()

    @pl.when(f < n_fsdp - 1)
    def _():
        right(0, norm, f).start()

    @pl.when(f > 0)
    def _():
        left(0, norm, f).start()

    img_pushes, txt_pushes = [], []
    for k in range(1, n_fsdp):
        img_pushes.append(push(img, gimg.at[f], img_s.at[k - 1], img_r.at[k - 1], fsdp=(f + k) % n_fsdp))
    for k in range(1, n_dp):
        txt_pushes.append(push(txt, ctxt.at[d], txt_s.at[k - 1], txt_r.at[k - 1], dp=(d + k) % n_dp))
    for copy in img_pushes + txt_pushes:
        copy.start()
    scatter(norm, f)
    keep[0].wait()
    expand(norm, f)

    for copy in keep[2:4] + img_pushes + txt_pushes:
        copy.wait()
    images = gimg[...].reshape(n_fsdp * pairs, -1)
    texts = ctxt[...].reshape(n_dp * pairs, -1)
    image_rows, image_codes = images[:, :embed_width], images[:, embed_width:]
    text_rows, text_codes = texts[:, :embed_width], texts[:, embed_width:]

    def weigh(left_rows, left_codes, right_rows, right_codes):
        logits = temper[...] * nt_dot(left_rows, right_rows) + offset[...]
        labels = jnp.where(nt_dot(left_codes, right_codes) == 0.0, 1.0, -1.0)
        return (temper[...] * -labels * jax.nn.sigmoid(-labels * logits)).astype(jnp.bfloat16)

    weights = weigh(image_rows, image_codes, text_rows, text_codes)
    image_part = jnp.dot(weights, text_rows, preferred_element_type=jnp.float32)
    crit[...] = jnp.zeros_like(crit)
    for p in range(n_fsdp):
        imgs[p] = image_part[p * pairs : (p + 1) * pairs].astype(jnp.bfloat16)
        crit[p, 0:1, :] = image_part[p * pairs : p * pairs + 1]
    weights = weigh(text_rows, text_codes, image_rows, image_codes)
    text_part = jnp.dot(weights, image_rows, preferred_element_type=jnp.float32)
    for p in range(n_dp):
        txts[p] = text_part[p * pairs : (p + 1) * pairs].astype(jnp.bfloat16)

    for h in range(1, n_fsdp):

        @pl.when(f - h >= 0)
        def _():
            b = f - h
            right(h - 1, norm, b).wait_recv()

            @pl.when(f < n_fsdp - 1)
            def _():
                right(h, grp.at[b], b).start()

            scatter(grp.at[b], b)

        @pl.when(f + h <= n_fsdp - 1)
        def _():
            b = f + h
            left(h - 1, norm, b).wait_recv()

            @pl.when(f > 0)
            def _():
                left(h, grp.at[b], b).start()

            scatter(grp.at[b], b)

        @pl.when(f - h >= 0)
        def _():
            expand(grp.at[f - h], f - h)

        @pl.when(f + h <= n_fsdp - 1)
        def _():
            expand(grp.at[f + h], f + h)

    critical, late = [], []
    for k in range(1, n_fsdp):
        peer = (f + k) % n_fsdp
        critical.append(push(crit.at[peer], crit_in.at[k - 1], cri_s.at[k - 1], cri_r.at[k - 1], fsdp=peer))
        late.append(push(imgs.at[peer], imgs_in.at[k - 1], ims_s.at[k - 1], ims_r.at[k - 1], fsdp=peer))
    for k in range(1, n_dp):
        peer = (d + k) % n_dp
        late.append(push(all_act.at[d], all_act.at[d], act_s.at[k - 1], act_r.at[k - 1], dp=peer))
        late.append(push(txts.at[peer], txts_in.at[k - 1], txs_s.at[k - 1], txs_r.at[k - 1], dp=peer))

    totals = jnp.concatenate([all_act[d, b] for b in range(n_fsdp)], axis=0) / (SIDE * SIDE)
    high = totals.astype(jnp.bfloat16)
    low = (totals - high.astype(jnp.float32)).astype(jnp.bfloat16)
    both = jnp.concatenate([high.astype(jnp.float32), low.astype(jnp.float32)], axis=0).astype(jnp.bfloat16)
    keep[4].wait()

    def mean_tile(i, carry):
        cols = pl.ds(pl.multiple_of(i * 256, 256), 256)
        product = jnp.dot(both, down[:, cols], preferred_element_type=jnp.float32)
        partial[:, cols] = product[:n_fsdp] + product[n_fsdp:]
        return carry

    lax.fori_loop(0, channels // 256, mean_tile, 0)
    for p in range(n_fsdp):
        for i in range(channels // embed_width):
            crit[p, i + 1 : i + 2, :] = partial[p : p + 1, i * embed_width : (i + 1) * embed_width]
    for copy in critical + late:
        copy.start()
    for copy in critical:
        copy.wait()
    total = crit[f]
    for k in range(1, n_fsdp):
        total = total + crit_in[k - 1]
    lines[...] = total
    image_row = lines[0:1, :]
    block_mean = jnp.concatenate(
        [lines[i + 1 : i + 2, :] for i in range(channels // embed_width)], axis=1
    )
    pooled = means[...] + scale[...] * block_mean
    centred = pooled - jnp.mean(pooled, axis=1, keepdims=True)
    inverse = 1.0 / jnp.sqrt(jnp.mean(centred * centred, axis=1, keepdims=True) + 1e-06)
    head_norm = centred * inverse
    head_out = head_norm * gain[...] + bias[...]
    keep[5].wait()
    embed = jnp.dot(
        jnp.broadcast_to(head_out, (16, channels)).astype(jnp.bfloat16),
        proj[...],
        preferred_element_type=jnp.float32,
    )[0:1]
    embed_len = jnp.sqrt(jnp.sum(embed * embed, axis=1, keepdims=True) + 1e-06)
    embed_unit = embed / embed_len
    inner_prod = jnp.sum(embed_unit * image_row, axis=1, keepdims=True)
    embed_grad = (image_row - embed_unit * inner_prod) / embed_len
    head_grad = lax.dot_general(
        jnp.broadcast_to(embed_grad, (16, embed_width)).astype(jnp.bfloat16),
        proj[...],
        (((1,), (1,)), ((), ())),
        preferred_element_type=jnp.float32,
    )[0:1]
    norm_grad = head_grad * gain[...]
    pool_grad = inverse * (
        norm_grad
        - jnp.mean(norm_grad, axis=1, keepdims=True)
        - head_norm * jnp.mean(norm_grad * head_norm, axis=1, keepdims=True)
    )
    row = (scale[...] * pool_grad / (SIDE * SIDE)).astype(jnp.bfloat16).astype(jnp.float32)
    for i in range(channels // 128):
        all_grad[d, f, i : i + 1, :] = row[:, i * 128 : (i + 1) * 128]
    grads = []
    for k in range(1, n_fsdp):
        grads.append(push(all_grad.at[d, f], all_grad.at[d, f], gra_s.at[k - 1], gra_r.at[k - 1], fsdp=(f + k) % n_fsdp))
    for copy in grads:
        copy.start()
    for copy in grads:
        copy.wait()
    group_grads = []
    for k in range(1, n_dp):
        group_grads.append(push(all_grad.at[d], all_grad.at[d], grd_s.at[k - 1], grd_r.at[k - 1], dp=(d + k) % n_dp))
    for copy in group_grads:
        copy.start()

    for b in range(n_fsdp):
        for k in range(2, n_dp, 2):
            slope_copy(k, b).wait_recv()
            onward(k, b).start()
    for copy in late:
        copy.wait()
    total = imgs[f].astype(jnp.float32)
    for k in range(1, n_fsdp):
        total = total + imgs_in[k - 1].astype(jnp.float32)
    img_sum[...] = total
    total = txts[d].astype(jnp.float32)
    for k in range(1, n_dp):
        total = total + txts_in[k - 1].astype(jnp.float32)
    txt_sum[...] = total
    keep[1].wait()
    for copy in group_grads:
        copy.wait()
    for h in range(n_fsdp - 1):

        @pl.when((f - h >= 0) & (f < n_fsdp - 1))
        def _():
            right(h, norm, f - h).wait_send()

        @pl.when((f + h <= n_fsdp - 1) & (f > 0))
        def _():
            left(h, norm, f + h).wait_send()

    for b in range(n_fsdp):
        slope_copy(0, b).wait()
        slope_keep(b).wait()
        for k in range(2, n_dp, 2):
            slope_copy(k, b).wait_send()
            onward(k, b).wait()
        if spread:
            for k in range(1, n_dp):
                column_copy(k, norm, b).wait()
            pltpu.make_async_copy(columns(norm, d), own.at[d, b], col_l.at[b]).wait()


def run_whole(n_dp, n_fsdp, normed, img_b, txt_b, temper, offset, means, scale, gain, bias, w_up, w_down, w_proj):
    channels, embed_width = w_proj.shape
    rows = normed.shape[0]
    hid_width = w_up.shape[1]
    pairs = img_b.shape[0]
    share = channels // n_dp
    dma = pltpu.SemaphoreType.DMA
    f32, half = jnp.float32, normed.dtype
    shape = jax.ShapeDtypeStruct
    lines = -(-(1 + channels // embed_width) // 8) * 8
    return pl.pallas_call(
        functools.partial(whole_kernel, n_dp, n_fsdp, share % 128 == 0),
        out_shape=(
            shape((n_fsdp, rows, channels), half),
            shape((n_dp, n_fsdp, rows, share), half),
            shape((n_dp, n_fsdp, rows, hid_width), half),
            shape((n_dp, n_fsdp, channels // 128, 128), f32),
            shape((n_dp, n_fsdp, 1, hid_width), f32),
            shape((pairs, embed_width), f32),
            shape((pairs, embed_width), f32),
        ),
        in_specs=[VMEM] * 9 + [ANY] * 3,
        out_specs=(VMEM, VMEM, ANY, VMEM, VMEM, VMEM, VMEM),
        scratch_shapes=[
            pltpu.VMEM(w_up.shape, half),
            pltpu.VMEM(w_down.shape, half),
            pltpu.VMEM(w_proj.shape, half),
            pltpu.VMEM((n_fsdp, *img_b.shape), half),
            pltpu.VMEM((n_dp, *txt_b.shape), half),
            pltpu.VMEM((n_fsdp, rows, hid_width), half),
            pltpu.VMEM((n_fsdp, lines, embed_width), f32),
            pltpu.VMEM((n_fsdp, pairs, embed_width), half),
            pltpu.VMEM((n_dp, pairs, embed_width), half),
            pltpu.VMEM((n_fsdp - 1, lines, embed_width), f32),
            pltpu.VMEM((n_fsdp - 1, pairs, embed_width), half),
            pltpu.VMEM((n_dp - 1, pairs, embed_width), half),
            pltpu.VMEM((lines, embed_width), f32),
            pltpu.VMEM((n_fsdp, channels), f32),
            dma((6,)),
        ]
        + [dma((n_dp - 1,))] * 2
        + [dma((n_fsdp - 1,))] * 2
        + [dma((n_fsdp,))] * 4
        + [dma((n_fsdp, n_dp - 1))] * 2
        + [dma((n_fsdp,))] * 2
        + [dma((n_fsdp, n_dp // 2))] * 4
        + [dma((n_fsdp - 1,))] * 4
        + [dma((n_dp - 1,))] * 4
        + [dma((n_fsdp - 1,))] * 2
        + [dma((n_dp - 1,))] * 2,
        compiler_params=pltpu.CompilerParams(
            collective_id=0, has_side_effects=True, vmem_limit_bytes=60 << 20
        ),
    )(normed, img_b, txt_b, temper, offset, means, scale, gain, bias, w_up, w_down, w_proj)


def id_columns(ids, sign, flip):
    high, low, one = sign * 256 * (ids // 256), sign * (ids % 256), jnp.ones_like(ids)
    codes = [one, one, high, low] if flip else [high, low, one, one]
    return jnp.pad(jnp.stack(codes, axis=1).astype(jnp.bfloat16), ((0, 0), (0, 124)))


def split_two(values):
    high = lax.reduce_precision(values, 8, 7)
    low = values - high
    return high.astype(jnp.bfloat16), low.astype(jnp.bfloat16)


def on_device(
    img_emb,
    txt_emb,
    img_ids,
    txt_ids,
    temp_log,
    logit_bias,
    block_in,
    dw_kernel,
    ln_gain,
    ln_bias,
    w_up,
    w_down,
    layer_scale,
    head_gain,
    head_bias,
    w_proj,
):
    channels = block_in.shape[1]
    hid_width = w_up.shape[1]
    patches = SIDE * SIDE
    n_dp, n_fsdp = lax.axis_size("dp"), lax.axis_size("fsdp")
    temper = jnp.exp(temp_log[0])
    offset = logit_bias[0]
    img_unit, img_len = unit_rows(img_emb)
    txt_unit, txt_len = unit_rows(txt_emb)
    img_b = jnp.concatenate([img_unit.astype(jnp.bfloat16), id_columns(img_ids, 1, False)], axis=1)
    txt_b = jnp.concatenate([txt_unit.astype(jnp.bfloat16), id_columns(txt_ids, -1, True)], axis=1)
    pictures = block_in.astype(jnp.float32).reshape(1, SIDE, SIDE, channels)
    mixed_rows = depthwise(pictures, dw_kernel).reshape(patches, channels)
    normed = layer_norm(mixed_rows, ln_gain, ln_bias)[0].astype(jnp.bfloat16)
    patch_means = jnp.mean(pictures, axis=(1, 2)).astype(jnp.bfloat16)
    group_blocks, own_normed, all_slope, all_grad, all_active, image_sum, text_sum = run_whole(
        n_dp,
        n_fsdp,
        normed,
        img_b,
        txt_b,
        temper.reshape(1, 1),
        offset.reshape(1, 1),
        patch_means.astype(jnp.float32).reshape(1, channels),
        layer_scale[None],
        head_gain[None],
        head_bias[None],
        w_up,
        w_down,
        w_proj,
    )
    group_normed = group_blocks.reshape(-1, channels)
    share = channels // n_dp
    if share % 128 == 0:
        own_normed = own_normed.reshape(-1, share)
    else:
        own_normed = lax.all_to_all(group_normed, "dp", split_axis=1, concat_axis=0, tiled=True)
    all_grad = all_grad.reshape(n_dp * n_fsdp, channels).astype(jnp.bfloat16)
    all_active = all_active.reshape(n_dp * n_fsdp, hid_width)
    row_down = jnp.dot(all_grad, w_down.T, preferred_element_type=jnp.float32)
    hid_grad = (
        (all_slope.reshape(n_dp * n_fsdp, patches, hid_width).astype(jnp.float32) * row_down[:, None, :])
        .astype(jnp.bfloat16)
        .reshape(-1, hid_width)
    )
    w_up_grad = lax.dot_general(
        own_normed, hid_grad, (((0,), (0,)), ((), ())), preferred_element_type=jnp.float32
    )
    own_grad = lax.dynamic_slice_in_dim(all_grad, lax.axis_index("dp") * share, share, 1)
    high, low = split_two(all_active)
    w_down_grad = lax.dot_general(
        jnp.concatenate([high, low]),
        jnp.concatenate([own_grad, own_grad]),
        (((0,), (0,)), ((), ())),
        preferred_element_type=jnp.float32,
    )
    img_grad = back_unit(image_sum, img_unit, img_len)
    txt_grad = back_unit(text_sum, txt_unit, txt_len)
    return (img_grad, txt_grad, w_up_grad, w_down_grad)


def solution(mesh):
    in_specs = (
        P(("dp", "fsdp"), None),
        P(("dp", "fsdp"), None),
        P(("dp", "fsdp")),
        P(("dp", "fsdp")),
        P(),
        P(),
        P(("dp", "fsdp"), None),
        P(),
        P(),
        P(),
        P(None, "fsdp"),
        P("fsdp", None),
        P(),
        P(),
        P(),
        P(),
    )
    out_specs = (P(("dp", "fsdp"), None), P(("dp", "fsdp"), None), P("dp", "fsdp"), P("fsdp", "dp"))
    return jax.shard_map(
        on_device, mesh=mesh, in_specs=in_specs, out_specs=out_specs, check_vma=False
    )
```

profile of v0, /device:TPU:0, one launch (start us, length us, event | category | flops | bytes accessed | tf_op | source)
XLA Modules:
  0.0 122.2 jit_solution(13910240619653267204)
XLA Ops:
  0.7 1.5 %fusion.129 = (f32[1,3072]{1,0:T(1,128)S(1)}, f32[1,3072]{1,0:T(1,128)S(1)}, f32[1,3072]{1,0:T(1,128)S(1)}, f32[1,3072]{1,0:T(1,128)S(1)}, f32[1,3072]{1,0:T(1,1...) fusion(f32[49,3072]{1,0:T(8,128)} %param.23), kind=kLoop, calls=%fused_computation.213 | loop fusion | bytes 270336 | tf_op jit(solution)/shard_map/slice | solution.py:33
  2.2 2.1 %fusion.127 = (f32[1,3072]{1,0:T(1,128)S(1)}, f32[1,3072]{1,0:T(1,128)S(1)}, f32[1,3072]{1,0:T(1,128)S(1)}, f32[1,3072]{1,0:T(1,128)S(1)}, f32[1,3072]{1,0:T(1,1...) fusion(f32[49,3072]{1,0:T(8,128)} %param.23), kind=kLoop, calls=%fused_computation.211 | loop fusion | bytes 466944 | tf_op jit(solution)/shard_map/slice | solution.py:33
  4.3 1.9 %fusion.128 = (f32[1,3072]{1,0:T(1,128)S(1)}, f32[1,3072]{1,0:T(1,128)S(1)}, f32[1,3072]{1,0:T(1,128)S(1)}, f32[1,3072]{1,0:T(1,128)S(1)}, f32[1,3072]{1,0:T(1,1...) fusion(f32[49,3072]{1,0:T(8,128)} %param.23), kind=kLoop, calls=%fused_computation.212 | loop fusion | bytes 466944 | tf_op jit(solution)/shard_map/slice | solution.py:33
  6.2 1.1 convert_bitcast_fusion
  7.2 5.5 %fusion.125 = (f32[8,8]{1,0:T(8,128)S(1)}, f32[1,8,8,3072]{3,2,1,0:T(8,128)S(1)}) fusion(f32[3072]{0:T(1024)S(1)} %bitcast.106, f32[3072]{0:T(1024)S(1)} %bitcast.107, f32[3072]{0:T(1024)S(1)} %bitcast.110, f32[3072]{0:T(1024)S(1)} %bitcast.111, f32[3072]{0:T(1024)S(1)} %bitcast.112, f32[3072]{0:T(1024)S(1)} %bitcast.113, f32[3072]{0:T(1024)S(1)} %bitcast.114, ...), kind=kLoop, calls=%fused_computation.210 | loop fusion | flops 19267520 | bytes 2175232 | tf_op jit(solution)/shard_map/reduce_sum | solution.py:40
  12.7 0.2 multiply_reduce_fusion
  13.2 1.7 %fusion.100.norm = bf16[64,3072]{1,0:T(8,128)(2,1)} fusion(f32[1,8,8,3072]{3,2,1,0:T(8,128)S(1)} %get-tuple-element.17, f32[3072]{0:T(1024)} %param.25, f32[3072]{0:T(1024)} %param.24, f32[64]{0:T(128)S(1)} %sqrt.22, f32[64]{0:T(128)S(1)} %div.65), kind=kLoop, calls=%fused_computation.152 | loop fusion | flops 983040 | bytes 1204736 | tf_op jit(solution)/shard_map/convert_element_type | solution.py:459
  14.9 0.1 copy.24
  15.0 0.1 fusion.108
  15.2 0.6 fusion.110.img
  16.0 0.1 fusion.109
  16.2 0.6 fusion.111.txt
  18.3 0.6 fusion.115
  18.9 81.1 %shard_map.183 = (bf16[4,64,3072]{2,1,0:T(8,128)(2,1)}, bf16[8,4,64,384]{3,2,1,0:T(8,128)(2,1)}, bf16[8,4,64,1536]{3,2,1,0:T(8,128)(2,1)}, f32[8,4,24,128]{3,2,1...) custom-call(bf16[64,3072]{1,0:T(8,128)(2,1)} %fusion.100.norm, ...), custom_call_target="tpu_custom_call" | custom-call | tf_op jit(solution)/shard_map/pallas_call | solution.py:371
  100.0 1.2 %multiply_reduce_fusion.2 = f32[32]{0:T(128)S(1)} fusion(f32[32,1024]{1,0:T(8,128)} %get-tuple-element.10, f32[32]{0:T(128)S(1)} %add_sqrt_fusion.1, bf16[32,1024]{1,0:T(8,128)(2,1)S(1)} %copy-done.2), kind=kLoop, calls=%fused_computation.174 | loop fusion | flops 131040 | bytes 196864 | tf_op jit(solution)/shard_map/reduce_sum | solution.py:21
  101.2 1.7 %subtract_divide_fusion.1 = f32[32,1024]{1,0:T(8,128)} fusion(f32[32,1024]{1,0:T(8,128)} %get-tuple-element.10, f32[32]{0:T(128)S(1)} %multiply_reduce_fusion.2, f32[32]{0:T(128)S(1)} %add_sqrt_fusion.1, bf16[32,1024]{1,0:T(8,128)(2,1)S(1)} %copy-done.2), kind=kLoop, calls=%fused_computation.173 | loop fusion | flops 163840 | bytes 327936 | tf_op jit(solution)/shard_map/div | solution.py:22
  102.9 1.1 multiply_reduce_fusion.1
  104.0 1.7 %subtract_divide_fusion = f32[32,1024]{1,0:T(8,128)} fusion(f32[32,1024]{1,0:T(8,128)} %get-tuple-element.11, f32[32]{0:T(128)S(1)} %multiply_reduce_fusion.1, f32[32]{0:T(128)S(1)} %add_sqrt_fusion, bf16[32,1024]{1,0:T(8,128)(2,1)S(1)} %copy-done.3), kind=kLoop, calls=%fused_computation.171 | loop fusion | flops 163840 | bytes 327936 | tf_op jit(solution)/shard_map/div | solution.py:22
  105.7 1.0 convert_element_type.92
  106.7 6.7 %fusion.124 = f32[32,1536]{1,0:T(8,128)S(1)} fusion(bf16[1536,3072]{1,0:T(8,128)(2,1)} %down_hbm.1, bf16[4,8,24,128]{3,2,1,0:T(8,128)(2,1)S(1)} %bitcast.94), kind=kOutput, calls=%fused_computation.209 | convolution fusion | flops 301989888 | bytes 9830400 | tf_op jit(solution)/shard_map/dot_general | solution.py:485
  113.5 2.0 %fusion = bf16[32,64,1536]{2,1,0:T(8,128)(2,1)S(1)} fusion(bf16[8,4,64,1536]{3,2,1,0:T(8,128)(2,1)S(1)} %bitcast.92, f32[32,1536]{1,0:T(8,128)S(1)} %fusion.124), kind=kLoop, calls=%fused_computation.49 | loop fusion | flops 9437184 | bytes 12779520 | tf_op jit(solution)/shard_map/convert_element_type | solution.py:488
  115.5 4.0 %fusion.130 = f32[384,1536]{1,0:T(8,128)} fusion(bf16[2048,384]{1,0:T(8,128)(2,1)S(1)} %bitcast.93, bf16[2048,1536]{1,0:T(8,128)(2,1)S(1)} %bitcast.90), kind=kOutput, calls=%fused_computation.214 | convolution fusion | flops 2415919104 | bytes 10223616 | tf_op jit(solution)/shard_map/dot_general | solution.py:491
  119.6 0.5 reduce.4
  120.3 1.9 %fusion.102 = f32[1536,384]{1,0:T(8,128)} fusion(bf16[32,1536]{1,0:T(8,128)(2,1)S(1)} %get-tuple-element.68, bf16[32,1536]{1,0:T(8,128)(2,1)S(1)} %get-tuple-element.67, bf16[32,384]{1,0:T(8,128)(2,1)S(1)} %constant_dynamic-slice_fusion), kind=kOutput, calls=%fused_computation.158 | convolution fusion | flops 75988992 | bytes 2580480 | tf_op jit(solution)/shard_map/dot_general | solution.py:496
  (36 shorter events, 0.8 us)
Async XLA Ops:
  0.6 17.5 %copy-start.1 = (bf16[64,3072]{1,0:T(8,128)(2,1)S(1)}, bf16[64,3072]{1,0:T(8,128)(2,1)}, u32[]{:S(2)}) copy-start(bf16[64,3072]{1,0:T(8,128)(2,1)} %param.22) | copy-start | bytes 1179652
  0.6 14.2 %copy-start.5 = (s32[32]{0:T(128)S(1)}, s32[32]{0:T(128)}, u32[]{:S(2)}) copy-start(s32[32]{0:T(128)} %param.19) | copy-start | bytes 388
  0.7 14.2 %copy-start.6 = (s32[32]{0:T(128)S(1)}, s32[32]{0:T(128)}, u32[]{:S(2)}) copy-start(s32[32]{0:T(128)} %param.18) | copy-start | bytes 388
  0.7 14.3 %copy-start.2 = (bf16[32,1024]{1,0:T(8,128)(2,1)S(1)}, bf16[32,1024]{1,0:T(8,128)(2,1)}, u32[]{:S(2)}) copy-start(bf16[32,1024]{1,0:T(8,128)(2,1)} %param.16) | copy-start | bytes 196612
  0.7 15.3 %copy-start.3 = (bf16[32,1024]{1,0:T(8,128)(2,1)S(1)}, bf16[32,1024]{1,0:T(8,128)(2,1)}, u32[]{:S(2)}) copy-start(bf16[32,1024]{1,0:T(8,128)(2,1)} %param.17) | copy-start | bytes 196612
  100.0 13.5 %slice-start = ((s8[6291456]{0:T(1024)(128)(4,1)}), s8[4194304]{0:T(1024)(128)(4,1)S(1)}, s32[]{:S(2)}) async-start(s8[6291456]{0:T(1024)(128)(4,1)} %bitcast.91), calls=%async_computation | async-start | bytes 8388608
  106.7 6.7 %slice-start.1 = ((s8[6291456]{0:T(1024)(128)(4,1)}), s8[2097152]{0:T(1024)(128)(4,1)S(1)}, s32[]{:S(2)}) async-start(s8[6291456]{0:T(1024)(128)(4,1)} %bitcast.91), calls=%async_computation.1 | async-start | bytes 4194304
  113.5 2.0 %copy-start = (bf16[8,4,64,384]{3,2,1,0:T(8,128)(2,1)S(1)}, bf16[8,4,64,384]{3,2,1,0:T(8,128)(2,1)}, u32[]{:S(2)}) copy-start(bf16[8,4,64,384]{3,2,1,0:T(8,128)(2,1)} %get-tuple-element.12) | copy-start | bytes 4718596
  115.5 4.1 %copy-start.4 = (f32[8,4,1,1536]{3,2,1,0:T(1,128)S(1)}, f32[8,4,1,1536]{3,2,1,0:T(1,128)}, u32[]{:S(2)}) copy-start(f32[8,4,1,1536]{3,2,1,0:T(1,128)} %get-tuple-element.15) | copy-start | bytes 589828
where the time goes:
time: 123 us; the launch traced here: 122 us
  Pallas kernels  81.1 us (66%)
  other arithmetic  20.2 us (16%)
  matrix products  12.7 us (10%)
  local copies, waits for them, and re-layouts  6.01 us (5%)
  between operations  2.2 us (2%)
    pallas_call x1, Pallas kernels, run_whole(): pl.pallas_call(functools.partial(whole_kernel, n_dp, n_fsdp, share % 128...  81.1 us
    dot_general x1, matrix products, on_device(): row_down = jnp.dot(all_grad, w_down.T, preferred_element_type=jnp.float32)  6.7 us
    reduce_sum x1, other arithmetic, layer_norm(): centre = jnp.mean(values, axis=-1, keepdims=True)  5.51 us
    slice x3, local copies, waits for them, and re-layouts, depthwise(): kernel[above * KERNEL + across]  5.49 us
    dot_general x1, matrix products, on_device(): lax.dot_general(own_normed, hid_grad, (((0,), (0,)), ((), ())), preferred...  4.05 us
    div x2, other arithmetic, back_unit(): return (gradient - unit_part * inner_prod) / length  3.38 us

commit v1 on v0

v1 whole, which is shorter than its diff:
```python
import functools
import types

import jax
import jax.numpy as jnp
from jax import lax
from jax.experimental import pallas as pl
from jax.experimental.pallas import tpu as pltpu
from jax.sharding import PartitionSpec as P

KERNEL = 7
SIDE = 8


def unit_rows(matrix):
    values = matrix.astype(jnp.float32)
    length = jnp.sqrt(jnp.sum(values * values, axis=1, keepdims=True) + 1e-06)
    return (values / length, length)


def back_unit(gradient, unit_part, length):
    inner_prod = jnp.sum(unit_part * gradient, axis=1, keepdims=True)
    return (gradient - unit_part * inner_prod) / length


MESH = pl.DeviceIdType.MESH
VMEM = pl.BlockSpec(memory_space=pltpu.VMEM)
ANY = pl.BlockSpec(memory_space=pl.ANY)


def push(source, target, send_sem, recv_sem, **peer):
    return pltpu.make_async_remote_copy(
        src_ref=source,
        dst_ref=target,
        send_sem=send_sem,
        recv_sem=recv_sem,
        device_id=peer,
        device_id_type=MESH,
    )


def second_parts(x):
    cubic = 0.044715
    slant = 0.7978845608028654
    square = x * x
    t = jnp.tanh(slant * x * (1.0 + cubic * square))
    half = 0.5 * (1.0 + t)
    slope = half + 0.5 * x * (1.0 - t * t) * slant * (1.0 + 3.0 * cubic * square)
    return x * half, slope


def nt_dot(left, right):
    return lax.dot_general(
        left, right, (((1,), (1,)), ((), ())), preferred_element_type=jnp.float32
    )


def depthwise_norm(block, kernel, gain, bias, mixed, normed, means):
    rows, channels = block.shape
    reach = KERNEL // 2

    def tile(i, total):
        cols = pl.ds(pl.multiple_of(i * 128, 128), 128)
        grid = block[:, cols].astype(jnp.float32).reshape(SIDE, SIDE, 128)
        means[:, cols] = jnp.sum(jnp.sum(grid, axis=0), axis=0, keepdims=True) / rows
        spot = lax.broadcasted_iota(jnp.int32, (SIDE, SIDE, 128), 1)
        lines = [jnp.zeros((SIDE, 128), jnp.float32) for _ in range(SIDE)]
        for across in range(KERNEL):
            step = across - reach
            if step == 0:
                moved = grid
            else:
                moved = pltpu.roll(grid, (-step) % SIDE, axis=1)
                moved = jnp.where((spot + step >= 0) & (spot + step < SIDE), moved, 0.0)
            for above in range(KERNEL):
                k = above * KERNEL + across
                weight = jnp.broadcast_to(kernel[k : k + 1, cols], (SIDE, 128))
                for r in range(max(0, reach - above), min(SIDE, SIDE + reach - above)):
                    lines[r] = lines[r] + weight * moved[r + above - reach]
        result = jnp.concatenate(lines, axis=0)
        mixed[:, cols] = result
        return total + result

    total = lax.fori_loop(0, channels // 128, tile, jnp.zeros((rows, 128), jnp.float32))
    centre = jnp.sum(total, axis=1, keepdims=True) / channels

    def spread(i, total):
        cols = pl.ds(pl.multiple_of(i * 128, 128), 128)
        centred = mixed[:, cols] - centre
        return total + centred * centred

    total = lax.fori_loop(0, channels // 128, spread, jnp.zeros((rows, 128), jnp.float32))
    inverse = 1.0 / jnp.sqrt(jnp.sum(total, axis=1, keepdims=True) / channels + 1e-06)

    def finish(i, carry):
        cols = pl.ds(pl.multiple_of(i * 128, 128), 128)
        normal = (mixed[:, cols] - centre) * inverse
        normed[:, cols] = (normal * gain[:, cols] + bias[:, cols]).astype(normed.dtype)
        return carry

    lax.fori_loop(0, channels // 128, finish, 0)


def whole_kernel(n_dp, n_fsdp, spread, names, *refs):
    v = types.SimpleNamespace(**dict(zip(names, refs)))
    block, img_emb, txt_emb = v.block, v.img_emb, v.txt_emb
    up, down, proj, grp, gimg, ctxt = v.up, v.down, v.proj, v.grp, v.gimg, v.ctxt
    norm, slope, crit, crit_in = v.norm, v.slope, v.crit, v.crit_in
    all_slope, all_act, all_grad = v.all_slope, v.all_act, v.all_grad
    d, f = lax.axis_index("dp"), lax.axis_index("fsdp")
    rows, channels = norm.shape
    share = channels // n_dp
    embed_width = proj.shape[1]
    hid_width = up.shape[1]
    pairs = img_emb.shape[0]
    chips = n_dp // 2
    core, chip = d % 2, d // 2
    partner = d + 1 - 2 * core
    multi = chips == 4
    images = n_dp * n_fsdp

    def flip(*masks):
        return d + sum(mask - 2 * mask * ((d // mask) % 2) for mask in masks)

    loc = v.loc
    keep_up = pltpu.make_async_copy(v.up_hbm, up, loc.at[0])
    keep_down = pltpu.make_async_copy(v.down_hbm, down, loc.at[1])
    keep_proj = pltpu.make_async_copy(v.proj_hbm, proj, loc.at[2])
    keep_norm = pltpu.make_async_copy(norm, grp.at[f], loc.at[3])
    for copy in (keep_up, keep_down, keep_proj):
        copy.start()
    barrier = pltpu.get_barrier_semaphore()
    for k in range(1, n_dp):
        pl.semaphore_signal(barrier, inc=1, device_id={"dp": (d + k) % n_dp}, device_id_type=MESH)
    for k in range(1, n_fsdp):
        pl.semaphore_signal(barrier, inc=1, device_id={"fsdp": (f + k) % n_fsdp}, device_id_type=MESH)

    depthwise_norm(block, v.kernel, v.ln_gain, v.ln_bias, v.mixed, norm, v.means)
    pl.semaphore_wait(barrier, n_dp + n_fsdp - 2)

    def right(h, source, b):
        return push(source, grp.at[b], v.rgt_s.at[h], v.rgt_r.at[h], fsdp=f + 1)

    def left(h, source, b):
        return push(source, grp.at[b], v.lft_s.at[h], v.lft_r.at[h], fsdp=f - 1)

    @pl.when(f < n_fsdp - 1)
    def _():
        right(0, norm, f).start()

    @pl.when(f > 0)
    def _():
        left(0, norm, f).start()

    keep_norm.start()

    def columns(source, owner):
        return source.at[:, pl.ds(pl.multiple_of(owner * share, 128), share)]

    def column_copy(k, source, b):
        peer = (d + k) % n_dp
        return push(columns(source, peer), v.own.at[d, b], v.col_s.at[b, k - 1], v.col_r.at[b, k - 1], dp=peer)

    def column_keep(source, b):
        return pltpu.make_async_copy(columns(source, d), v.own.at[d, b], v.col_l.at[b])

    def scatter(source, b):
        if spread:
            for k in range(1, n_dp):
                column_copy(k, source, b).start()
            column_keep(source, b).start()

    def near(j, b):
        source, target = slope.at[b], all_slope.at[d, b]
        peer = flip(2 << j) if multi else (d + 2 * j + 2) % n_dp
        return push(source, target, v.slo_s.at[b, j], v.slo_r.at[b, j], dp=peer)

    def from_near(j):
        return flip(2 << j) if multi else (d - 2 * j - 2 + n_dp) % n_dp

    n_near = 2 if multi else chips - 1

    def half(j, b):
        spot = all_slope.at[flip(2 << j), b, pl.ds(j * (rows // 2), rows // 2)]
        return push(spot, spot, v.hlf_s.at[b, j], v.hlf_r.at[b, j], dp=flip(4 >> j))

    def to_partner(j, b):
        if j == 0:
            source, target = slope.at[b], all_slope.at[d, b]
        else:
            origin = flip(2, 4) if multi and j == 3 else from_near(j - 1)
            source = target = all_slope.at[origin, b]
        return push(source, target, v.par_s.at[b, j], v.par_r.at[b, j], dp=partner)

    def slope_keep(b):
        return pltpu.make_async_copy(slope.at[b], all_slope.at[d, b], v.slo_l.at[b])

    def relay(b):
        for j in range(n_near):
            near(j, b).wait_recv()
            if multi:
                half(j, b).start()
            to_partner(j + 1, b).start()

    wide = 256 if hid_width % 256 == 0 else 128

    def expand(source, b):
        def tile(i, carry):
            cols = pl.ds(pl.multiple_of(i * wide, wide), wide)
            hidden = jnp.dot(source[...], up[:, cols], preferred_element_type=jnp.float32)
            active, slant = second_parts(hidden)
            slope[b, :, cols] = slant.astype(jnp.bfloat16)
            active = active.astype(jnp.bfloat16).astype(jnp.float32)
            all_act[d, b, :, cols] = jnp.sum(active, axis=0, keepdims=True)
            return carry

        lax.fori_loop(0, hid_width // wide, tile, 0)
        for j in range(n_near):
            near(j, b).start()
        to_partner(0, b).start()
        slope_keep(b).start()

    for source, codes, spot in (
        (img_emb, v.img_codes, gimg.at[f]),
        (txt_emb, v.txt_codes, ctxt.at[d]),
    ):
        spot[:, :embed_width] = unit_rows(source[...])[0].astype(jnp.bfloat16)
        spot[:, embed_width:] = codes[...]
    img_pushes = [
        push(gimg.at[f], gimg.at[f], v.img_s.at[k - 1], v.img_r.at[k - 1], fsdp=(f + k) % n_fsdp)
        for k in range(1, n_fsdp)
    ]

    def chip_copies(ref, name):
        out = [
            push(ref.at[d], ref.at[d], getattr(v, name + "_s").at[j - 1], getattr(v, name + "_r").at[j - 1], dp=(d + 2 * j) % n_dp)
            for j in range(1, chips)
        ]
        out_near = push(ref.at[d], ref.at[d], getattr(v, name + "p_s").at[0], getattr(v, name + "p_r").at[0], dp=partner)
        onward = []
        for j in range(1, chips):
            spot = ref.at[(d + n_dp - 2 * j) % n_dp]
            onward.append(push(spot, spot, getattr(v, name + "p_s").at[j], getattr(v, name + "p_r").at[j], dp=partner))
        return out + [out_near], onward

    def forward(copies, onward):
        for copy, more in zip(copies, onward):
            copy.wait_recv()
            more.start()

    def settle(copies, onward):
        for copy in copies[: chips - 1]:
            copy.wait_send()
        copies[chips - 1].wait()
        for copy in onward:
            copy.wait()

    txt_copies, txt_onward = chip_copies(ctxt, "txt")
    for copy in img_pushes + txt_copies:
        copy.start()
    keep_up.wait()
    expand(norm, f)
    scatter(norm, f)

    def score():
        forward(txt_copies, txt_onward)
        for copy in img_pushes:
            copy.wait()
        settle(txt_copies, txt_onward)
        images_all = gimg[...].reshape(n_fsdp * pairs, -1)
        texts_all = ctxt[...].reshape(n_dp * pairs, -1)
        image_rows, image_codes = images_all[:, :embed_width], images_all[:, embed_width:]
        text_rows, text_codes = texts_all[:, :embed_width], texts_all[:, embed_width:]
        temper = jnp.exp(v.temper[...])
        offset = v.offset[...]

        def weigh(left_rows, left_codes, right_rows, right_codes):
            logits = temper * nt_dot(left_rows, right_rows) + offset
            labels = jnp.where(nt_dot(left_codes, right_codes) == 0.0, 1.0, -1.0)
            return (temper * -labels * jax.nn.sigmoid(-labels * logits)).astype(jnp.bfloat16)

        weights = weigh(image_rows, image_codes, text_rows, text_codes)
        image_part = jnp.dot(weights, text_rows, preferred_element_type=jnp.float32)
        piece = crit.shape[2]
        for p in range(n_fsdp):
            v.imgs[p] = image_part[p * pairs : (p + 1) * pairs].astype(jnp.bfloat16)
            for i in range(embed_width // piece):
                crit[p, i : i + 1, :] = image_part[p * pairs : p * pairs + 1, i * piece : (i + 1) * piece]
        weights = weigh(text_rows, text_codes, image_rows, image_codes)
        text_part = jnp.dot(weights, image_rows, preferred_element_type=jnp.float32)
        for p in range(n_dp):
            v.txts[p % 2, p // 2] = text_part[p * pairs : (p + 1) * pairs].astype(jnp.bfloat16)
        pair_copy.start()

    pair_copy = push(v.txts.at[1 - core], v.txts_pair, v.txx_s.at[0], v.txx_r.at[0], dp=partner)

    for h in range(1, n_fsdp):

        @pl.when(f - h >= 0)
        def _():
            b = f - h
            right(h - 1, norm, b).wait_recv()

            @pl.when(f < n_fsdp - 1)
            def _():
                right(h, grp.at[b], b).start()

        @pl.when(f + h <= n_fsdp - 1)
        def _():
            b = f + h
            left(h - 1, norm, b).wait_recv()

            @pl.when(f > 0)
            def _():
                left(h, grp.at[b], b).start()

        @pl.when(f - h >= 0)
        def _():
            expand(grp.at[f - h], f - h)

        @pl.when(f + h <= n_fsdp - 1)
        def _():
            expand(grp.at[f + h], f + h)

        if h == 1:
            relay(f)
        else:

            @pl.when(f - h + 1 >= 0)
            def _():
                relay(f - h + 1)

            @pl.when(f + h - 1 <= n_fsdp - 1)
            def _():
                relay(f + h - 1)

        @pl.when(f - h >= 0)
        def _():
            scatter(grp.at[f - h], f - h)

        @pl.when(f + h <= n_fsdp - 1)
        def _():
            scatter(grp.at[f + h], f + h)

        if h == 1:
            score()

    act_copies, act_onward = chip_copies(all_act, "act")
    critical, late = [], []
    for k in range(1, n_fsdp):
        peer = (f + k) % n_fsdp
        critical.append(push(crit.at[peer], crit_in.at[k - 1], v.cri_s.at[k - 1], v.cri_r.at[k - 1], fsdp=peer))
        late.append(push(v.imgs.at[peer], v.imgs_in.at[k - 1], v.ims_s.at[k - 1], v.ims_r.at[k - 1], fsdp=peer))

    totals = jnp.concatenate([all_act[d, b] for b in range(n_fsdp)], axis=0) / (SIDE * SIDE)
    high = totals.astype(jnp.bfloat16)
    low = (totals - high.astype(jnp.float32)).astype(jnp.bfloat16)
    both = jnp.concatenate([high.astype(jnp.float32), low.astype(jnp.float32)], axis=0).astype(jnp.bfloat16)
    keep_down.wait()
    partial = v.partial

    def mean_tile(i, carry):
        cols = pl.ds(pl.multiple_of(i * 256, 256), 256)
        product = jnp.dot(both, down[:, cols], preferred_element_type=jnp.float32)
        partial[:, cols] = product[:n_fsdp] + product[n_fsdp:]
        return carry

    lax.fori_loop(0, channels // 256, mean_tile, 0)
    piece = crit.shape[2]
    first = embed_width // piece
    for p in range(n_fsdp):
        for i in range(channels // piece):
            crit[p, first + i : first + i + 1, :] = partial[p : p + 1, i * piece : (i + 1) * piece]
    for copy in critical + late + act_copies:
        copy.start()

    pair_copy.wait()
    texts_own = v.txts[core].astype(jnp.float32) + v.txts_pair[...].astype(jnp.float32)
    v.txts_sum[...] = texts_own.astype(jnp.bfloat16)
    text_copies = []
    for j in range(1, chips):
        text_copies.append(
            push(
                v.txts_sum.at[(chip + j) % chips],
                v.txts_in.at[j - 1],
                v.txs_s.at[j - 1],
                v.txs_r.at[j - 1],
                dp=(d + 2 * j) % n_dp,
            )
        )
    for copy in text_copies:
        copy.start()

    for copy in critical:
        copy.wait()
    total = crit[f]
    for k in range(1, n_fsdp):
        total = total + crit_in[k - 1]
    lines = v.lines
    lines[...] = total
    image_row = jnp.concatenate([lines[i : i + 1, :] for i in range(first)], axis=1)
    block_mean = jnp.concatenate([lines[first + i : first + i + 1, :] for i in range(channels // piece)], axis=1)
    scale, gain, bias = v.scale, v.gain, v.bias
    patch_means = v.means[...].astype(jnp.bfloat16).astype(jnp.float32)
    pooled = patch_means + scale[...] * block_mean
    centred = pooled - jnp.mean(pooled, axis=1, keepdims=True)
    inverse = 1.0 / jnp.sqrt(jnp.mean(centred * centred, axis=1, keepdims=True) + 1e-06)
    head_norm = centred * inverse
    head_out = head_norm * gain[...] + bias[...]
    keep_proj.wait()
    embed = jnp.dot(
        jnp.broadcast_to(head_out, (16, channels)).astype(jnp.bfloat16),
        proj[...],
        preferred_element_type=jnp.float32,
    )[0:1]
    embed_len = jnp.sqrt(jnp.sum(embed * embed, axis=1, keepdims=True) + 1e-06)
    embed_unit = embed / embed_len
    inner_prod = jnp.sum(embed_unit * image_row, axis=1, keepdims=True)
    embed_grad = (image_row - embed_unit * inner_prod) / embed_len
    head_grad = lax.dot_general(
        jnp.broadcast_to(embed_grad, (16, embed_width)).astype(jnp.bfloat16),
        proj[...],
        (((1,), (1,)), ((), ())),
        preferred_element_type=jnp.float32,
    )[0:1]
    norm_grad = head_grad * gain[...]
    pool_grad = inverse * (
        norm_grad
        - jnp.mean(norm_grad, axis=1, keepdims=True)
        - head_norm * jnp.mean(norm_grad * head_norm, axis=1, keepdims=True)
    )
    row = scale[...] * pool_grad / (SIDE * SIDE)
    for i in range(channels // 128):
        v.grow[i : i + 1, :] = row[:, i * 128 : (i + 1) * 128]
    all_grad[d, f] = v.grow[...].astype(jnp.bfloat16)
    grads = []
    for k in range(1, n_fsdp):
        grads.append(
            push(all_grad.at[d, f], all_grad.at[d, f], v.gra_s.at[k - 1], v.gra_r.at[k - 1], fsdp=(f + k) % n_fsdp)
        )
    for copy in grads:
        copy.start()

    @pl.when(f == n_fsdp - 1)
    def _():
        relay(0)

    @pl.when(f == 0)
    def _():
        relay(n_fsdp - 1)

    for copy in grads:
        copy.wait()
    grd_copies, grd_onward = chip_copies(all_grad, "grd")
    for copy in grd_copies:
        copy.start()
    forward(act_copies, act_onward)
    forward(grd_copies, grd_onward)
    if multi:
        for b in range(n_fsdp):
            for j in range(2):
                half(j, b).wait_recv()
            to_partner(3, b).start()
    for copy in late + text_copies:
        copy.wait()
    total = v.imgs[f].astype(jnp.float32)
    for k in range(1, n_fsdp):
        total = total + v.imgs_in[k - 1].astype(jnp.float32)
    v.img_sum[...] = total
    total = v.txts[core, chip].astype(jnp.float32) + v.txts_pair[chip].astype(jnp.float32)
    for j in range(1, chips):
        total = total + v.txts_in[j - 1].astype(jnp.float32)
    v.txt_sum[...] = total
    settle(grd_copies, grd_onward)
    v.gwide[...] = all_grad[...].astype(jnp.float32).reshape(images, channels // 128, 128)
    for i in range(channels // 128):
        v.gmat[:, i * 128 : (i + 1) * 128] = v.gwide[:, i, :].astype(jnp.bfloat16)

    def down_tile(i, carry):
        spot = pl.ds(pl.multiple_of(i * wide, wide), wide)
        v.row_down[:, spot] = nt_dot(v.gmat[...], down[spot, :])
        return carry

    lax.fori_loop(0, hid_width // wide, down_tile, 0)
    settle(act_copies, act_onward)
    keep_norm.wait()
    for h in range(n_fsdp - 1):

        @pl.when((f - h >= 0) & (f < n_fsdp - 1))
        def _():
            right(h, norm, f - h).wait_send()

        @pl.when((f + h <= n_fsdp - 1) & (f > 0))
        def _():
            left(h, norm, f + h).wait_send()

    for b in range(n_fsdp):
        if spread:
            for k in range(1, n_dp):
                column_copy(k, norm, b).wait()
            column_keep(norm, b).wait()
        slope_keep(b).wait()
        for j in range(n_near):
            near(j, b).wait_send()
            if multi:
                half(j, b).wait_send()
        for j in range(chips):
            to_partner(j, b).wait()


def run_whole(n_dp, n_fsdp, args, w_up, w_down, w_proj):
    channels, embed_width = w_proj.shape
    rows = args["block"].shape[0]
    hid_width = w_up.shape[1]
    pairs = args["img_emb"].shape[0]
    share = channels // n_dp
    chips = n_dp // 2
    images = n_dp * n_fsdp
    spread = share % 128 == 0
    dma = pltpu.SemaphoreType.DMA
    f32, half = jnp.float32, jnp.bfloat16
    shape = jax.ShapeDtypeStruct
    width = embed_width + args["img_codes"].shape[1]
    piece = (channels + embed_width) // 8
    outs = dict(
        all_slope=(shape((n_dp, n_fsdp, rows, hid_width), half), ANY),
        gmat=(shape((images, channels), half), VMEM),
        row_down=(shape((images, hid_width), f32), VMEM),
        all_act=(shape((n_dp, n_fsdp, 1, hid_width), f32), VMEM),
        img_sum=(shape((pairs, embed_width), f32), VMEM),
        txt_sum=(shape((pairs, embed_width), f32), VMEM),
    )
    scratch = dict(
        up=pltpu.VMEM(w_up.shape, half),
        down=pltpu.VMEM(w_down.shape, half),
        proj=pltpu.VMEM(w_proj.shape, half),
        mixed=pltpu.VMEM((rows, channels), f32),
        norm=pltpu.VMEM((rows, channels), half),
        means=pltpu.VMEM((1, channels), f32),
        gimg=pltpu.VMEM((n_fsdp, pairs, width), half),
        ctxt=pltpu.VMEM((n_dp, pairs, width), half),
        slope=pltpu.VMEM((n_fsdp, rows, hid_width), half),
        all_grad=pltpu.VMEM((n_dp, n_fsdp, channels // 128, 128), half),
        gwide=pltpu.VMEM((images, channels // 128, 128), f32),
        grow=pltpu.VMEM((channels // 128, 128), f32),
        crit=pltpu.VMEM((n_fsdp, 8, piece), f32),
        crit_in=pltpu.VMEM((n_fsdp - 1, 8, piece), f32),
        lines=pltpu.VMEM((8, piece), f32),
        partial=pltpu.VMEM((n_fsdp, channels), f32),
        imgs=pltpu.VMEM((n_fsdp, pairs, embed_width), half),
        imgs_in=pltpu.VMEM((n_fsdp - 1, pairs, embed_width), half),
        txts=pltpu.VMEM((2, chips, pairs, embed_width), half),
        txts_pair=pltpu.VMEM((chips, pairs, embed_width), half),
        txts_sum=pltpu.VMEM((chips, pairs, embed_width), half),
        txts_in=pltpu.VMEM((chips - 1, pairs, embed_width), half),
    )
    if spread:
        outs.update(own=(shape((n_dp, n_fsdp, rows, share), half), ANY))
        scratch.update(grp=pltpu.VMEM((n_fsdp, rows, channels), half))
    else:
        outs.update(grp=(shape((n_fsdp, rows, channels), half), VMEM))
    sems = dict(
        loc=(4,),
        rgt=(n_fsdp,),
        lft=(n_fsdp,),
        col=(n_fsdp, n_dp - 1),
        slo=(n_fsdp, chips - 1),
        hlf=(n_fsdp, 2),
        par=(n_fsdp, chips),
        img=(n_fsdp - 1,),
        txt=(chips - 1,),
        txtp=(chips,),
        act=(chips - 1,),
        actp=(chips,),
        grd=(chips - 1,),
        grdp=(chips,),
        gra=(n_fsdp - 1,),
        cri=(n_fsdp - 1,),
        ims=(n_fsdp - 1,),
        txs=(chips - 1,),
        txx=(1,),
    )
    for name, dims in sems.items():
        if name == "loc":
            scratch[name] = dma(dims)
        else:
            scratch[name + "_s"] = dma(dims)
            scratch[name + "_r"] = dma(dims)
    scratch.update(col_l=dma((n_fsdp,)))
    scratch.update(slo_l=dma((n_fsdp,)))
    names = [*args, "up_hbm", "down_hbm", "proj_hbm", *outs, *scratch]
    results = pl.pallas_call(
        functools.partial(whole_kernel, n_dp, n_fsdp, spread, names),
        out_shape=[one for one, _ in outs.values()],
        in_specs=[VMEM] * len(args) + [ANY] * 3,
        out_specs=[spec for _, spec in outs.values()],
        scratch_shapes=list(scratch.values()),
        compiler_params=pltpu.CompilerParams(
            collective_id=0, has_side_effects=True, vmem_limit_bytes=60 << 20
        ),
    )(*args.values(), w_up, w_down, w_proj)
    return types.SimpleNamespace(**dict(zip(outs, results)))


def finish_kernel(
    img_emb, txt_emb, img_sum, txt_sum, act, gmat, row_down, own_hbm, slope_hbm,
    img_grad, txt_grad, up_hbm, down_hbm,
    own, own_t, slopes, hid, up, downs, sems, out_sems,
):
    tiles, all_rows, wide = slopes.shape
    images = gmat.shape[0]
    patches = all_rows // images
    share = own.shape[1]
    hid_width = tiles * wide
    own_copy = pltpu.make_async_copy(own_hbm, own, sems.at[tiles])
    own_copy.start()

    def fetch(i):
        return pltpu.make_async_copy(slope_hbm.at[:, pl.ds(i * wide, wide)], slopes.at[i], sems.at[i])

    for i in range(tiles):
        fetch(i).start()
    for source, summed, result in ((img_emb, img_sum, img_grad), (txt_emb, txt_sum, txt_grad)):
        unit_part, length = unit_rows(source[...])
        result[...] = back_unit(summed[...], unit_part, length)
    d = lax.axis_index("dp")
    own_grad = gmat[:, pl.ds(pl.multiple_of(d * share, 128), share)]
    totals = jnp.concatenate([act[i] for i in range(images)], axis=0)
    high = totals.astype(jnp.bfloat16)
    low = (totals - high.astype(jnp.float32)).astype(jnp.bfloat16)
    both = jnp.concatenate([high, low], axis=0)
    grads = jnp.concatenate([own_grad, own_grad], axis=0)
    downs[...] = lax.dot_general(both, grads, (((0,), (0,)), ((), ())), preferred_element_type=jnp.float32)
    down_out = pltpu.make_async_copy(downs, down_hbm, out_sems.at[tiles])
    down_out.start()
    own_copy.wait()
    own_t[...] = own[...].T

    def emit(i):
        return pltpu.make_async_copy(up.at[i], up_hbm.at[:, pl.ds(i * wide, wide)], out_sems.at[i])

    for i in range(tiles):
        fetch(i).wait()
        for k in range(images):
            spot = pl.ds(k * patches, patches)
            factor = row_down[k : k + 1, i * wide : (i + 1) * wide]
            hid[spot, :] = (slopes[i, spot, :].astype(jnp.float32) * factor).astype(jnp.bfloat16)
        up[i] = jnp.dot(own_t[...], hid[...], preferred_element_type=jnp.float32)
        emit(i).start()
    down_out.wait()
    for i in range(tiles):
        emit(i).wait()


def run_finish(img_emb, txt_emb, got):
    n_dp, n_fsdp, rows, share = got.own.shape
    hid_width = got.row_down.shape[1]
    images, channels = got.gmat.shape
    all_rows = images * rows
    wide = 256 if hid_width % 256 == 0 else 128
    tiles = hid_width // wide
    f32, half = jnp.float32, jnp.bfloat16
    shape = jax.ShapeDtypeStruct
    return pl.pallas_call(
        finish_kernel,
        out_shape=(
            shape(img_emb.shape, f32),
            shape(txt_emb.shape, f32),
            shape((share, hid_width), f32),
            shape((hid_width, share), f32),
        ),
        in_specs=[VMEM] * 7 + [ANY] * 2,
        out_specs=(VMEM, VMEM, ANY, ANY),
        scratch_shapes=[
            pltpu.VMEM((all_rows, share), half),
            pltpu.VMEM((share, all_rows), half),
            pltpu.VMEM((tiles, all_rows, wide), half),
            pltpu.VMEM((all_rows, wide), half),
            pltpu.VMEM((tiles, share, wide), f32),
            pltpu.VMEM((hid_width, share), f32),
            pltpu.SemaphoreType.DMA((tiles + 1,)),
            pltpu.SemaphoreType.DMA((tiles + 1,)),
        ],
        compiler_params=pltpu.CompilerParams(vmem_limit_bytes=40 << 20),
    )(
        img_emb,
        txt_emb,
        got.img_sum,
        got.txt_sum,
        got.all_act.reshape(images, 1, hid_width),
        got.gmat,
        got.row_down,
        got.own.reshape(all_rows, share),
        got.all_slope.reshape(all_rows, hid_width),
    )


def id_columns(ids, sign, flip):
    high, low, one = sign * 256 * (ids // 256), sign * (ids % 256), jnp.ones_like(ids)
    codes = [one, one, high, low] if flip else [high, low, one, one]
    return jnp.pad(jnp.stack(codes, axis=1).astype(jnp.bfloat16), ((0, 0), (0, 124)))


def split_two(values):
    high = lax.reduce_precision(values, 8, 7)
    low = values - high
    return high.astype(jnp.bfloat16), low.astype(jnp.bfloat16)


def on_device(
    img_emb,
    txt_emb,
    img_ids,
    txt_ids,
    temp_log,
    logit_bias,
    block_in,
    dw_kernel,
    ln_gain,
    ln_bias,
    w_up,
    w_down,
    layer_scale,
    head_gain,
    head_bias,
    w_proj,
):
    rows, channels = block_in.shape
    hid_width = w_up.shape[1]
    n_dp, n_fsdp = lax.axis_size("dp"), lax.axis_size("fsdp")
    args = dict(
        block=block_in,
        kernel=dw_kernel,
        ln_gain=ln_gain[None],
        ln_bias=ln_bias[None],
        img_emb=img_emb,
        txt_emb=txt_emb,
        img_codes=id_columns(img_ids, 1, False),
        txt_codes=id_columns(txt_ids, -1, True),
        temper=temp_log.reshape(1, 1),
        offset=logit_bias.reshape(1, 1),
        scale=layer_scale[None],
        gain=head_gain[None],
        bias=head_bias[None],
    )
    got = run_whole(n_dp, n_fsdp, args, w_up, w_down, w_proj)
    share = channels // n_dp
    if share % 128 == 0:
        return run_finish(img_emb, txt_emb, got)
    own_normed = lax.all_to_all(got.grp.reshape(-1, channels), "dp", split_axis=1, concat_axis=0, tiled=True)
    slopes = got.all_slope.reshape(n_dp * n_fsdp, rows, hid_width).astype(jnp.float32)
    hid_grad = (slopes * got.row_down[:, None, :]).astype(jnp.bfloat16).reshape(-1, hid_width)
    w_up_grad = lax.dot_general(
        own_normed, hid_grad, (((0,), (0,)), ((), ())), preferred_element_type=jnp.float32
    )
    own_grad = lax.dynamic_slice_in_dim(got.gmat, lax.axis_index("dp") * share, share, 1)
    high, low = split_two(got.all_act.reshape(n_dp * n_fsdp, hid_width))
    w_down_grad = lax.dot_general(
        jnp.concatenate([high, low]),
        jnp.concatenate([own_grad, own_grad]),
        (((0,), (0,)), ((), ())),
        preferred_element_type=jnp.float32,
    )
    img_unit, img_len = unit_rows(img_emb)
    txt_unit, txt_len = unit_rows(txt_emb)
    img_grad = back_unit(got.img_sum, img_unit, img_len)
    txt_grad = back_unit(got.txt_sum, txt_unit, txt_len)
    return (img_grad, txt_grad, w_up_grad, w_down_grad)


def solution(mesh):
    in_specs = (
        P(("dp", "fsdp"), None),
        P(("dp", "fsdp"), None),
        P(("dp", "fsdp")),
        P(("dp", "fsdp")),
        P(),
        P(),
        P(("dp", "fsdp"), None),
        P(),
        P(),
        P(),
        P(None, "fsdp"),
        P("fsdp", None),
        P(),
        P(),
        P(),
        P(),
    )
    out_specs = (P(("dp", "fsdp"), None), P(("dp", "fsdp"), None), P("dp", "fsdp"), P("fsdp", "dp"))
    return jax.shard_map(
        on_device, mesh=mesh, in_specs=in_specs, out_specs=out_specs, check_vma=False
    )
```

time: 123 us -> 95.4 us (0.78)
  other arithmetic: 20.2 us -> 0.7 us
  matrix products: 12.7 us -> 0 us
  local copies, waits for them, and re-layouts: 6.01 us -> 10.2 us
    dot_general x3 -> x0, matrix products: 12.7 us -> none  [the longest x1 6.7 us: on_device(): row_down = jnp.dot(all_grad, w_down.T, preferred_element_type=jnp.float32)]
    unnamed x19 -> x18, local copies, waits for them, and re-layouts: 0.08 us -> 8.78 us
    reduce_sum x7 -> x0, other arithmetic: 8.41 us -> none  [the longest x1 5.51 us: layer_norm(): centre = jnp.mean(values, axis=-1, keepdims=True)]
    convert_element_type x7 -> x0, other arithmetic: 5.52 us -> none  [the longest x1 2.01 us: on_device(): hid_grad = (all_slope.reshape(n_dp * n_fsdp, patches, hid_width).astype(j...]
    slice x3 -> x0, local copies, waits for them, and re-layouts: 5.49 us -> none  [depthwise(): kernel[above * KERNEL + across]]
    div x3 -> x0, other arithmetic: 3.39 us -> none  [the longest x2 3.38 us: back_unit(): return (gradient - unit_part * inner_prod) / length]
    concatenate x2 -> x0, other arithmetic: 1.28 us -> none  [the longest x1 0.64 us: on_device(): jnp.concatenate([txt_unit.astype(jnp.bfloat16), id_columns(txt_ids, -1, T...]
    pallas_call x1 -> x2, Pallas kernels: 81.1 us -> 82 us  [the longest x1 73.2 us: run_whole(): pl.pallas_call(functools.partial(whole_kernel, n_dp, n_fsdp, spread, name...]
where the time goes in v1:
time: 95.4 us; the launch traced here: 95 us
  Pallas kernels  82 us (86%)
  local copies, waits for them, and re-layouts  10.2 us (11%)
  between operations  2.14 us (2%)
    pallas_call x1, Pallas kernels, run_whole(): pl.pallas_call(functools.partial(whole_kernel, n_dp, n_fsdp, spread, name...  73.2 us
    pallas_call x1, Pallas kernels, run_finish(): pl.pallas_call(finish_kernel, out_shape=(shape(img_emb.shape, f32), shape...  8.84 us
    unnamed x18, local copies, waits for them, and re-layouts  8.78 us

profile of v1, /device:TPU:0, one launch (start us, length us, event | category | flops | bytes accessed | tf_op | source)
XLA Modules:
  0.0 95.0 jit_solution(11043717804294028599)
XLA Ops:
  1.9 0.7 convert_bitcast_fusion
  2.6 0.1 copy.25
  2.7 0.6 pad.8.refs_7_
  3.4 0.1 copy.24
  3.5 0.6 pad.7.refs_6_
  4.1 0.0 copy-start.2
  4.1 0.0 copy-start.3
  4.1 73.2 %shard_map.183 = (bf16[8,4,64,1536]{3,2,1,0:T(8,128)(2,1)}, bf16[32,3072]{1,0:T(8,128)(2,1)}, f32[32,1536]{1,0:T(8,128)}, f32[8,4,1,1536]{3,2,1,0:T(1,128)}, f32...) custom-call(bf16[64,3072]{1,0:T(8,128)(2,1)} %refs_0_.1, f32[49,3072]{1,0:T(8,128)} %refs_1_.1, ...), custom_call_target="tpu_custom_call" | custom-call | tf_op jit(solution)/shard_map/pallas_call | solution.py:592
  77.2 0.0 copy-done.2
  77.2 0.0 copy-done.3
  77.3 0.0 copy-start
  77.3 2.8 %copy-done = bf16[8,4,64,1536]{3,2,1,0:T(8,128)(2,1)S(1)} copy-done((bf16[8,4,64,1536]{3,2,1,0:T(8,128)(2,1)S(1)}, bf16[8,4,64,1536]{3,2,1,0:T(8,128)(2,1)}, u32[]{:S(2)}) %copy-start) | copy-done | bytes 6291480
  80.0 0.0 copy-start.1
  80.0 1.4 %copy-done.1 = bf16[8,4,64,384]{3,2,1,0:T(8,128)(2,1)S(1)} copy-done((bf16[8,4,64,384]{3,2,1,0:T(8,128)(2,1)S(1)}, bf16[8,4,64,384]{3,2,1,0:T(8,128)(2,1)}, u32[]{:S(2)}) %copy-start.1) | copy-done | bytes 1572888
  81.5 0.0 copy-start.4
  81.5 0.9 copy-done.4
  82.4 0.0 copy-start.5
  82.4 0.9 copy-done.5
  83.3 0.0 copy-start.6
  83.3 0.9 copy-done.6
  84.2 0.0 copy-start.7
  84.2 0.9 copy-done.7
  85.1 0.9 copy-done.8
  86.0 8.8 %shard_map.184 = (f32[32,1024]{1,0:T(8,128)}, f32[32,1024]{1,0:T(8,128)}, f32[384,1536]{1,0:T(8,128)}, f32[1536,384]{1,0:T(8,128)}) custom-call(bf16[32,1024]{1,0:T(8,128)(2,1)S(1)} %copy-done.2, bf16[32,1024]{1,0:T(8,128)(2,1)S(1)} %copy-done.3, f32[32,1024]{1,0:T(8,128)S(1)} %copy-done.7, f32[32,1024]{1,0:T(8,128)S(1)} %copy-done.8, ...), custom_call_target="tpu_custom_call" | custom-call | tf_op jit(solution)/shard_map/pallas_call | solution.py:664
  (3 shorter events, 0.0 us)
Async XLA Ops:
  4.1 73.2 %copy-start.2 = (bf16[32,1024]{1,0:T(8,128)(2,1)S(1)}, bf16[32,1024]{1,0:T(8,128)(2,1)}, u32[]{:S(2)}) copy-start(bf16[32,1024]{1,0:T(8,128)(2,1)} %img_emb.1) | copy-start | bytes 196612
  4.1 73.2 %copy-start.3 = (bf16[32,1024]{1,0:T(8,128)(2,1)S(1)}, bf16[32,1024]{1,0:T(8,128)(2,1)}, u32[]{:S(2)}) copy-start(bf16[32,1024]{1,0:T(8,128)(2,1)} %txt_emb.1) | copy-start | bytes 196612
  77.3 2.8 %copy-start = (bf16[8,4,64,1536]{3,2,1,0:T(8,128)(2,1)S(1)}, bf16[8,4,64,1536]{3,2,1,0:T(8,128)(2,1)}, u32[]{:S(2)}) copy-start(bf16[8,4,64,1536]{3,2,1,0:T(8,128)(2,1)} %get-tuple-element.17) | copy-start | bytes 18874372
  80.0 1.4 %copy-start.1 = (bf16[8,4,64,384]{3,2,1,0:T(8,128)(2,1)S(1)}, bf16[8,4,64,384]{3,2,1,0:T(8,128)(2,1)}, u32[]{:S(2)}) copy-start(bf16[8,4,64,384]{3,2,1,0:T(8,128)(2,1)} %get-tuple-element.16) | copy-start | bytes 4718596
  81.5 0.9 copy-start.4
  82.4 0.9 copy-start.5
  83.3 0.9 copy-start.6
  84.2 0.9 copy-start.7
  85.1 0.9 copy-start.8

commit v2 on v1

--- a/solution.py
+++ b/solution.py
@@ -26,6 +26,7 @@
 MESH = pl.DeviceIdType.MESH
 VMEM = pl.BlockSpec(memory_space=pltpu.VMEM)
 ANY = pl.BlockSpec(memory_space=pl.ANY)
+HBM = pl.BlockSpec(memory_space=pltpu.HBM)
 
 
 def push(source, target, send_sem, recv_sem, **peer):
@@ -53,6 +54,22 @@
     return lax.dot_general(
         left, right, (((1,), (1,)), ((), ())), preferred_element_type=jnp.float32
     )
+
+
+def id_codes(ids, sign, flip, width):
+    pairs = ids.shape[1]
+    diagonal = lax.broadcasted_iota(jnp.int32, (pairs, pairs), 0) == lax.broadcasted_iota(jnp.int32, (pairs, pairs), 1)
+    spot = lax.broadcasted_iota(jnp.int32, (pairs, width), 1)
+
+    def column(values):
+        return jnp.sum(jnp.where(diagonal, (sign * values).astype(jnp.float32), 0.0), axis=1, keepdims=True)
+
+    low = ids & 255
+    first = 2 if flip else 0
+    ones = (spot >= 2 - first) & (spot < 4 - first)
+    codes = jnp.where(ones, 1.0, 0.0)
+    codes = jnp.where(spot == first, column(ids - low), codes)
+    return jnp.where(spot == first + 1, column(low), codes).astype(jnp.bfloat16)
 
 
 def depthwise_norm(block, kernel, gain, bias, mixed, normed, means):
@@ -101,7 +118,7 @@
     lax.fori_loop(0, channels // 128, finish, 0)
 
 
-def whole_kernel(n_dp, n_fsdp, spread, names, *refs):
+def whole_kernel(n_dp, n_fsdp, spread, names, small, *refs):
     v = types.SimpleNamespace(**dict(zip(names, refs)))
     block, img_emb, txt_emb = v.block, v.img_emb, v.txt_emb
     up, down, proj, grp, gimg, ctxt = v.up, v.down, v.proj, v.grp, v.gimg, v.ctxt
@@ -123,18 +140,25 @@
         return d + sum(mask - 2 * mask * ((d // mask) % 2) for mask in masks)
 
     loc = v.loc
+    fetches = [
+        pltpu.make_async_copy(getattr(v, name + "_hbm"), getattr(v, name), v.first.at[i])
+        for i, name in enumerate(small)
+    ]
+    for copy in fetches:
+        copy.start()
     keep_up = pltpu.make_async_copy(v.up_hbm, up, loc.at[0])
     keep_down = pltpu.make_async_copy(v.down_hbm, down, loc.at[1])
     keep_proj = pltpu.make_async_copy(v.proj_hbm, proj, loc.at[2])
     keep_norm = pltpu.make_async_copy(norm, grp.at[f], loc.at[3])
-    for copy in (keep_up, keep_down, keep_proj):
-        copy.start()
+    keep_up.start()
     barrier = pltpu.get_barrier_semaphore()
     for k in range(1, n_dp):
         pl.semaphore_signal(barrier, inc=1, device_id={"dp": (d + k) % n_dp}, device_id_type=MESH)
     for k in range(1, n_fsdp):
         pl.semaphore_signal(barrier, inc=1, device_id={"fsdp": (f + k) % n_fsdp}, device_id_type=MESH)
 
+    for copy in fetches:
+        copy.wait()
     depthwise_norm(block, v.kernel, v.ln_gain, v.ln_bias, v.mixed, norm, v.means)
     pl.semaphore_wait(barrier, n_dp + n_fsdp - 2)
 
@@ -220,12 +244,12 @@
         to_partner(0, b).start()
         slope_keep(b).start()
 
-    for source, codes, spot in (
-        (img_emb, v.img_codes, gimg.at[f]),
-        (txt_emb, v.txt_codes, ctxt.at[d]),
+    for source, ids, sign, spot in (
+        (img_emb, v.img_ids, 1, gimg.at[f]),
+        (txt_emb, v.txt_ids, -1, ctxt.at[d]),
     ):
         spot[:, :embed_width] = unit_rows(source[...])[0].astype(jnp.bfloat16)
-        spot[:, embed_width:] = codes[...]
+        spot[:, embed_width:] = id_codes(ids[...], sign, sign < 0, spot.shape[1] - embed_width)
     img_pushes = [
         push(gimg.at[f], gimg.at[f], v.img_s.at[k - 1], v.img_r.at[k - 1], fsdp=(f + k) % n_fsdp)
         for k in range(1, n_fsdp)
@@ -259,6 +283,8 @@
     for copy in img_pushes + txt_copies:
         copy.start()
     keep_up.wait()
+    keep_down.start()
+    keep_proj.start()
     expand(norm, f)
     scatter(norm, f)
 
@@ -334,13 +360,15 @@
             def _():
                 relay(f + h - 1)
 
-        @pl.when(f - h >= 0)
-        def _():
-            scatter(grp.at[f - h], f - h)
-
-        @pl.when(f + h <= n_fsdp - 1)
-        def _():
-            scatter(grp.at[f + h], f + h)
+        if h < n_fsdp - 1:
+
+            @pl.when(f - h >= 0)
+            def _():
+                scatter(grp.at[f - h], f - h)
+
+            @pl.when(f + h <= n_fsdp - 1)
+            def _():
+                scatter(grp.at[f + h], f + h)
 
         if h == 1:
             score()
@@ -371,7 +399,7 @@
     for p in range(n_fsdp):
         for i in range(channels // piece):
             crit[p, first + i : first + i + 1, :] = partial[p : p + 1, i * piece : (i + 1) * piece]
-    for copy in critical + late + act_copies:
+    for copy in critical + act_copies:
         copy.start()
 
     pair_copy.wait()
@@ -438,24 +466,37 @@
         grads.append(
             push(all_grad.at[d, f], all_grad.at[d, f], v.gra_s.at[k - 1], v.gra_r.at[k - 1], fsdp=(f + k) % n_fsdp)
         )
-    for copy in grads:
+    for copy in grads + late:
         copy.start()
-
-    @pl.when(f == n_fsdp - 1)
-    def _():
-        relay(0)
-
-    @pl.when(f == 0)
-    def _():
-        relay(n_fsdp - 1)
-
     for copy in grads:
         copy.wait()
     grd_copies, grd_onward = chip_copies(all_grad, "grd")
     for copy in grd_copies:
         copy.start()
+
+    @pl.when(f == n_fsdp - 1)
+    def _():
+        relay(0)
+        scatter(grp.at[0], 0)
+
+    @pl.when(f == 0)
+    def _():
+        relay(n_fsdp - 1)
+        scatter(grp.at[n_fsdp - 1], n_fsdp - 1)
+
+    forward(grd_copies, grd_onward)
     forward(act_copies, act_onward)
-    forward(grd_copies, grd_onward)
+    settle(grd_copies, grd_onward)
+    v.gwide[...] = all_grad[...].astype(jnp.float32).reshape(images, channels // 128, 128)
+    for i in range(channels // 128):
+        v.gmat[:, i * 128 : (i + 1) * 128] = v.gwide[:, i, :].astype(jnp.bfloat16)
+
+    def down_tile(i, carry):
+        spot = pl.ds(pl.multiple_of(i * wide, wide), wide)
+        v.row_down[:, spot] = nt_dot(v.gmat[...], down[spot, :])
+        return carry
+
+    lax.fori_loop(0, hid_width // wide, down_tile, 0)
     if multi:
         for b in range(n_fsdp):
             for j in range(2):
@@ -471,17 +512,6 @@
     for j in range(1, chips):
         total = total + v.txts_in[j - 1].astype(jnp.float32)
     v.txt_sum[...] = total
-    settle(grd_copies, grd_onward)
-    v.gwide[...] = all_grad[...].astype(jnp.float32).reshape(images, channels // 128, 128)
-    for i in range(channels // 128):
-        v.gmat[:, i * 128 : (i + 1) * 128] = v.gwide[:, i, :].astype(jnp.bfloat16)
-
-    def down_tile(i, carry):
-        spot = pl.ds(pl.multiple_of(i * wide, wide), wide)
-        v.row_down[:, spot] = nt_dot(v.gmat[...], down[spot, :])
-        return carry
-
-    lax.fori_loop(0, hid_width // wide, down_tile, 0)
     settle(act_copies, act_onward)
     keep_norm.wait()
     for h in range(n_fsdp - 1):
@@ -520,7 +550,7 @@
     dma = pltpu.SemaphoreType.DMA
     f32, half = jnp.float32, jnp.bfloat16
     shape = jax.ShapeDtypeStruct
-    width = embed_width + args["img_codes"].shape[1]
+    width = embed_width + 128
     piece = (channels + embed_width) // 8
     outs = dict(
         all_slope=(shape((n_dp, n_fsdp, rows, hid_width), half), ANY),
@@ -588,41 +618,39 @@
             scratch[name + "_r"] = dma(dims)
     scratch.update(col_l=dma((n_fsdp,)))
     scratch.update(slo_l=dma((n_fsdp,)))
-    names = [*args, "up_hbm", "down_hbm", "proj_hbm", *outs, *scratch]
+    for name, one in args.items():
+        scratch[name] = pltpu.VMEM(one.shape, one.dtype)
+    scratch.update(first=dma((len(args),)))
+    inputs = [name + "_hbm" for name in [*args, "up", "down", "proj"]]
+    names = [*inputs, *outs, *scratch]
     results = pl.pallas_call(
-        functools.partial(whole_kernel, n_dp, n_fsdp, spread, names),
+        functools.partial(whole_kernel, n_dp, n_fsdp, spread, names, list(args)),
         out_shape=[one for one, _ in outs.values()],
-        in_specs=[VMEM] * len(args) + [ANY] * 3,
+        in_specs=[HBM] * (len(args) + 3),
         out_specs=[spec for _, spec in outs.values()],
         scratch_shapes=list(scratch.values()),
         compiler_params=pltpu.CompilerParams(
-            collective_id=0, has_side_effects=True, vmem_limit_bytes=60 << 20
+            collective_id=0, has_side_effects=True, vmem_limit_bytes=42 << 20
         ),
-    )(*args.values(), w_up, w_down, w_proj)
+    )(*[pltpu.with_memory_space_constraint(one, pltpu.HBM) if one.size > 1 else one for one in [*args.values(), w_up, w_down, w_proj]])
     return types.SimpleNamespace(**dict(zip(outs, results)))
 
 
 def finish_kernel(
-    img_emb, txt_emb, img_sum, txt_sum, act, gmat, row_down, own_hbm, slope_hbm,
+    img_hbm, txt_hbm, img_sum, txt_sum, act, gmat, row_down, own, slopes,
     img_grad, txt_grad, up_hbm, down_hbm,
-    own, own_t, slopes, hid, up, downs, sems, out_sems,
+    img_emb, txt_emb, own_t, hid, up, downs, sems, out_sems,
 ):
-    tiles, all_rows, wide = slopes.shape
+    img_copy = pltpu.make_async_copy(img_hbm, img_emb, sems.at[0])
+    txt_copy = pltpu.make_async_copy(txt_hbm, txt_emb, sems.at[1])
+    img_copy.start()
+    txt_copy.start()
+    tiles, _, wide = up.shape
+    all_rows = slopes.shape[0]
     images = gmat.shape[0]
     patches = all_rows // images
     share = own.shape[1]
     hid_width = tiles * wide
-    own_copy = pltpu.make_async_copy(own_hbm, own, sems.at[tiles])
-    own_copy.start()
-
-    def fetch(i):
-        return pltpu.make_async_copy(slope_hbm.at[:, pl.ds(i * wide, wide)], slopes.at[i], sems.at[i])
-
-    for i in range(tiles):
-        fetch(i).start()
-    for source, summed, result in ((img_emb, img_sum, img_grad), (txt_emb, txt_sum, txt_grad)):
-        unit_part, length = unit_rows(source[...])
-        result[...] = back_unit(summed[...], unit_part, length)
     d = lax.axis_index("dp")
     own_grad = gmat[:, pl.ds(pl.multiple_of(d * share, 128), share)]
     totals = jnp.concatenate([act[i] for i in range(images)], axis=0)
@@ -633,19 +661,27 @@
     downs[...] = lax.dot_general(both, grads, (((0,), (0,)), ((), ())), preferred_element_type=jnp.float32)
     down_out = pltpu.make_async_copy(downs, down_hbm, out_sems.at[tiles])
     down_out.start()
-    own_copy.wait()
     own_t[...] = own[...].T
+    img_copy.wait()
+    txt_copy.wait()
+    for source, summed, result in ((img_emb, img_sum, img_grad), (txt_emb, txt_sum, txt_grad)):
+        unit_part, length = unit_rows(source[...])
+        result[...] = back_unit(summed[...], unit_part, length)
 
     def emit(i):
         return pltpu.make_async_copy(up.at[i], up_hbm.at[:, pl.ds(i * wide, wide)], out_sems.at[i])
 
-    for i in range(tiles):
-        fetch(i).wait()
+    def weigh(i):
         for k in range(images):
             spot = pl.ds(k * patches, patches)
             factor = row_down[k : k + 1, i * wide : (i + 1) * wide]
-            hid[spot, :] = (slopes[i, spot, :].astype(jnp.float32) * factor).astype(jnp.bfloat16)
-        up[i] = jnp.dot(own_t[...], hid[...], preferred_element_type=jnp.float32)
+            hid[i % 2, spot, :] = (slopes[spot, i * wide : (i + 1) * wide].astype(jnp.float32) * factor).astype(jnp.bfloat16)
+
+    weigh(0)
+    for i in range(tiles):
+        if i + 1 < tiles:
+            weigh(i + 1)
+        up[i] = jnp.dot(own_t[...], hid[i % 2], preferred_element_type=jnp.float32)
         emit(i).start()
     down_out.wait()
     for i in range(tiles):
@@ -669,22 +705,22 @@
             shape((share, hid_width), f32),
             shape((hid_width, share), f32),
         ),
-        in_specs=[VMEM] * 7 + [ANY] * 2,
+        in_specs=[HBM] * 2 + [VMEM] * 7,
         out_specs=(VMEM, VMEM, ANY, ANY),
         scratch_shapes=[
-            pltpu.VMEM((all_rows, share), half),
+            pltpu.VMEM(img_emb.shape, half),
+            pltpu.VMEM(txt_emb.shape, half),
             pltpu.VMEM((share, all_rows), half),
-            pltpu.VMEM((tiles, all_rows, wide), half),
-            pltpu.VMEM((all_rows, wide), half),
+            pltpu.VMEM((2, all_rows, wide), half),
             pltpu.VMEM((tiles, share, wide), f32),
             pltpu.VMEM((hid_width, share), f32),
-            pltpu.SemaphoreType.DMA((tiles + 1,)),
+            pltpu.SemaphoreType.DMA((2,)),
             pltpu.SemaphoreType.DMA((tiles + 1,)),
         ],
-        compiler_params=pltpu.CompilerParams(vmem_limit_bytes=40 << 20),
+        compiler_params=pltpu.CompilerParams(vmem_limit_bytes=24 << 20),
     )(
-        img_emb,
-        txt_emb,
+        pltpu.with_memory_space_constraint(img_emb, pltpu.HBM),
+        pltpu.with_memory_space_constraint(txt_emb, pltpu.HBM),
         got.img_sum,
         got.txt_sum,
         got.all_act.reshape(images, 1, hid_width),
@@ -693,12 +729,6 @@
         got.own.reshape(all_rows, share),
         got.all_slope.reshape(all_rows, hid_width),
     )
-
-
-def id_columns(ids, sign, flip):
-    high, low, one = sign * 256 * (ids // 256), sign * (ids % 256), jnp.ones_like(ids)
-    codes = [one, one, high, low] if flip else [high, low, one, one]
-    return jnp.pad(jnp.stack(codes, axis=1).astype(jnp.bfloat16), ((0, 0), (0, 124)))
 
 
 def split_two(values):
@@ -735,8 +765,8 @@
         ln_bias=ln_bias[None],
         img_emb=img_emb,
         txt_emb=txt_emb,
-        img_codes=id_columns(img_ids, 1, False),
-        txt_codes=id_columns(txt_ids, -1, True),
+        img_ids=img_ids[None],
+        txt_ids=txt_ids[None],
         temper=temp_log.reshape(1, 1),
         offset=logit_bias.reshape(1, 1),
         scale=layer_scale[None],

time: 95.4 us -> 81.3 us (0.85)
  local copies, waits for them, and re-layouts: 10.2 us -> 0 us
  Pallas kernels: 82 us -> 79.2 us
    unnamed x18 -> x0, local copies, waits for them, and re-layouts: 8.78 us -> none
    pallas_call x1, Pallas kernels: 8.84 us -> 5.42 us  [run_finish(): pl.pallas_call(finish_kernel, out_shape=(shape(img_emb.shape, f32), shape...]
    pad x2 -> x0, local copies, waits for them, and re-layouts: 1.22 us -> none  [id_columns(): jnp.pad(jnp.stack(codes, axis=1).astype(jnp.bfloat16), ((0, 0), (0, 124)))]
where the time goes in v2:
time: 81.3 us; the launch traced here: 81.1 us
  Pallas kernels  79.2 us (97%)
  between operations  1.93 us (2%)
    pallas_call x1, Pallas kernels, run_whole(): pl.pallas_call(functools.partial(whole_kernel, n_dp, n_fsdp, spread, name...  73.8 us
    pallas_call x1, Pallas kernels, run_finish(): pl.pallas_call(finish_kernel, out_shape=(shape(img_emb.shape, f32), shape...  5.42 us

profile of v2, /device:TPU:0, one launch (start us, length us, event | category | flops | bytes accessed | tf_op | source)
XLA Modules:
  0.0 81.1 jit_solution(4377151556924051190)
XLA Ops:
  1.9 73.8 %shard_map.183 = (bf16[8,4,64,1536]{3,2,1,0:T(8,128)(2,1)S(1)}, bf16[32,3072]{1,0:T(8,128)(2,1)S(1)}, f32[32,1536]{1,0:T(8,128)S(1)}, f32[8,4,1,1536]{3,2,1,0:T(...) custom-call(bf16[64,3072]{1,0:T(8,128)(2,1)} %refs_0_.1, ...), custom_call_target="tpu_custom_call" | custom-call | tf_op jit(solution)/shard_map/pallas_call | solution.py:626
  75.7 5.4 %shard_map.184 = (f32[32,1024]{1,0:T(8,128)}, f32[32,1024]{1,0:T(8,128)}, f32[384,1536]{1,0:T(8,128)}, f32[1536,384]{1,0:T(8,128)}) custom-call(bf16[32,1024]{1,0:T(8,128)(2,1)} %img_hbm.1, bf16[32,1024]{1,0:T(8,128)(2,1)} %txt_hbm.1, f32[32,1024]{1,0:T(8,128)S(1)} %get-tuple-element.11.img_sum, f32[32,1024]{1,0:T(8,128)S(1)} %get-tuple-element.12.txt_sum, ...), custom_call_target="tpu_custom_call" | custom-call | tf_op jit(solution)/shard_map/pallas_call | solution.py:700

commit v3 on v2

--- a/solution.py
+++ b/solution.py
@@ -280,7 +280,7 @@
             copy.wait()
 
     txt_copies, txt_onward = chip_copies(ctxt, "txt")
-    for copy in img_pushes + txt_copies:
+    for copy in txt_copies:
         copy.start()
     keep_up.wait()
     keep_down.start()
@@ -340,6 +340,10 @@
             def _():
                 left(h, grp.at[b], b).start()
 
+        if h == 1:
+            for copy in img_pushes:
+                copy.start()
+
         @pl.when(f - h >= 0)
         def _():
             expand(grp.at[f - h], f - h)
@@ -370,7 +374,7 @@
             def _():
                 scatter(grp.at[f + h], f + h)
 
-        if h == 1:
+        if h == min(2, n_fsdp - 1):
             score()
 
     act_copies, act_onward = chip_copies(all_act, "act")
@@ -484,9 +488,21 @@
         relay(n_fsdp - 1)
         scatter(grp.at[n_fsdp - 1], n_fsdp - 1)
 
+    def diagonal(b):
+        for j in range(2):
+            half(j, b).wait_recv()
+        to_partner(3, b).start()
+
     forward(grd_copies, grd_onward)
     forward(act_copies, act_onward)
     settle(grd_copies, grd_onward)
+    if multi:
+        for b in range(n_fsdp):
+
+            @pl.when(((f != n_fsdp - 1) | (b != 0)) & ((f != 0) | (b != n_fsdp - 1)))
+            def _():
+                diagonal(b)
+
     v.gwide[...] = all_grad[...].astype(jnp.float32).reshape(images, channels // 128, 128)
     for i in range(channels // 128):
         v.gmat[:, i * 128 : (i + 1) * 128] = v.gwide[:, i, :].astype(jnp.bfloat16)
@@ -498,10 +514,15 @@
 
     lax.fori_loop(0, hid_width // wide, down_tile, 0)
     if multi:
-        for b in range(n_fsdp):
-            for j in range(2):
-                half(j, b).wait_recv()
-            to_partner(3, b).start()
+
+        @pl.when(f == n_fsdp - 1)
+        def _():
+            diagonal(0)
+
+        @pl.when(f == 0)
+        def _():
+            diagonal(n_fsdp - 1)
+
     for copy in late + text_copies:
         copy.wait()
     total = v.imgs[f].astype(jnp.float32)

time: 81.3 us -> 78.5 us (0.966)
  Pallas kernels: 79.2 us -> 76.4 us
    pallas_call x1, Pallas kernels: 73.8 us -> 71 us  [run_whole(): pl.pallas_call(functools.partial(whole_kernel, n_dp, n_fsdp, spread, name...]
where the time goes in v3:
time: 78.5 us; the launch traced here: 78.3 us
  Pallas kernels  76.4 us (97%)
  between operations  1.93 us (2%)
    pallas_call x1, Pallas kernels, run_whole(): pl.pallas_call(functools.partial(whole_kernel, n_dp, n_fsdp, spread, name...  71 us
    pallas_call x1, Pallas kernels, run_finish(): pl.pallas_call(finish_kernel, out_shape=(shape(img_emb.shape, f32), shape...  5.42 us

profile of v3, /device:TPU:0, one launch (start us, length us, event | category | flops | bytes accessed | tf_op | source)
XLA Modules:
  0.0 78.3 jit_solution(11364677266399369488)
XLA Ops:
  1.9 71.0 %shard_map.183 = (bf16[8,4,64,1536]{3,2,1,0:T(8,128)(2,1)S(1)}, bf16[32,3072]{1,0:T(8,128)(2,1)S(1)}, f32[32,1536]{1,0:T(8,128)S(1)}, f32[8,4,1,1536]{3,2,1,0:T(...) custom-call(bf16[64,3072]{1,0:T(8,128)(2,1)} %refs_0_.1, ...), custom_call_target="tpu_custom_call" | custom-call | tf_op jit(solution)/shard_map/pallas_call | solution.py:647
  72.9 5.4 %shard_map.184 = (f32[32,1024]{1,0:T(8,128)}, f32[32,1024]{1,0:T(8,128)}, f32[384,1536]{1,0:T(8,128)}, f32[1536,384]{1,0:T(8,128)}) custom-call(bf16[32,1024]{1,0:T(8,128)(2,1)} %img_hbm.1, bf16[32,1024]{1,0:T(8,128)(2,1)} %txt_hbm.1, f32[32,1024]{1,0:T(8,128)S(1)} %get-tuple-element.11.img_sum, f32[32,1024]{1,0:T(8,128)S(1)} %get-tuple-element.12.txt_sum, ...), custom_call_target="tpu_custom_call" | custom-call | tf_op jit(solution)/shard_map/pallas_call | solution.py:721

commit v4 on v3

--- a/solution.py
+++ b/solution.py
@@ -403,7 +403,7 @@
     for p in range(n_fsdp):
         for i in range(channels // piece):
             crit[p, first + i : first + i + 1, :] = partial[p : p + 1, i * piece : (i + 1) * piece]
-    for copy in critical + act_copies:
+    for copy in critical:
         copy.start()
 
     pair_copy.wait()
@@ -420,8 +420,6 @@
                 dp=(d + 2 * j) % n_dp,
             )
         )
-    for copy in text_copies:
-        copy.start()
 
     for copy in critical:
         copy.wait()
@@ -475,7 +473,7 @@
     for copy in grads:
         copy.wait()
     grd_copies, grd_onward = chip_copies(all_grad, "grd")
-    for copy in grd_copies:
+    for copy in grd_copies + act_copies + text_copies:
         copy.start()
 
     @pl.when(f == n_fsdp - 1)
@@ -494,7 +492,6 @@
         to_partner(3, b).start()
 
     forward(grd_copies, grd_onward)
-    forward(act_copies, act_onward)
     settle(grd_copies, grd_onward)
     if multi:
         for b in range(n_fsdp):
@@ -513,6 +510,7 @@
         return carry
 
     lax.fori_loop(0, hid_width // wide, down_tile, 0)
+    forward(act_copies, act_onward)
     if multi:
 
         @pl.when(f == n_fsdp - 1)

time: 78.5 us -> 80 us (1.019)
  Pallas kernels: 76.4 us -> 77.8 us
    pallas_call x1, Pallas kernels: 71 us -> 72.4 us  [run_whole(): pl.pallas_call(functools.partial(whole_kernel, n_dp, n_fsdp, spread, name...]
where the time goes in v4:
time: 80 us; the launch traced here: 79.8 us
  Pallas kernels  77.8 us (97%)
  between operations  1.93 us (2%)
    pallas_call x1, Pallas kernels, run_whole(): pl.pallas_call(functools.partial(whole_kernel, n_dp, n_fsdp, spread, name...  72.4 us
    pallas_call x1, Pallas kernels, run_finish(): pl.pallas_call(finish_kernel, out_shape=(shape(img_emb.shape, f32), shape...  5.42 us

profile of v4, /device:TPU:0, one launch (start us, length us, event | category | flops | bytes accessed | tf_op | source)
XLA Modules:
  0.0 79.8 jit_solution(15904825798099172860)
XLA Ops:
  1.9 72.4 %shard_map.183 = (bf16[8,4,64,1536]{3,2,1,0:T(8,128)(2,1)S(1)}, bf16[32,3072]{1,0:T(8,128)(2,1)S(1)}, f32[32,1536]{1,0:T(8,128)S(1)}, f32[8,4,1,1536]{3,2,1,0:T(...) custom-call(bf16[64,3072]{1,0:T(8,128)(2,1)} %refs_0_.1, ...), custom_call_target="tpu_custom_call" | custom-call | tf_op jit(solution)/shard_map/pallas_call | solution.py:645
  74.4 5.4 %shard_map.184 = (f32[32,1024]{1,0:T(8,128)}, f32[32,1024]{1,0:T(8,128)}, f32[384,1536]{1,0:T(8,128)}, f32[1536,384]{1,0:T(8,128)}) custom-call(bf16[32,1024]{1,0:T(8,128)(2,1)} %img_hbm.1, bf16[32,1024]{1,0:T(8,128)(2,1)} %txt_hbm.1, f32[32,1024]{1,0:T(8,128)S(1)} %get-tuple-element.11.img_sum, f32[32,1024]{1,0:T(8,128)S(1)} %get-tuple-element.12.txt_sum, ...), custom_call_target="tpu_custom_call" | custom-call | tf_op jit(solution)/shard_map/pallas_call | solution.py:719
